TPU v7x, 256 devices: a whole 4x4x8 slice. The times are simulated.
256 devices in a mesh: dp: 4 (over y), expert: 64 (over x, z, core).
Axes of the slice: x: 4, y: 4, z: 8, core: 2. Of those that a mesh axis runs over, the one named last changes fastest.
Arguments:
- tokens: bfloat16 [6144, 4096], P(('dp', 'expert')), may hold values from -6 to 6
- out_grad: bfloat16 [6144, 4096], P(('dp', 'expert')), may hold values from -6 to 6
- routes: int32 [6144, 8], P(('dp', 'expert')), may hold values from 0 to 63, all different within a row; in each aligned block of 24 rows (0 to 23, 24 to 47, ...) at most 4 rows name the same one
- gates: bfloat16 [6144, 8], P(('dp', 'expert')), may hold values from 0.099609375 to 0.5
- w_gate: bfloat16 [64, 768, 4096], P('expert', 'dp'), may hold values from -0.09375 to 0.09375
- w_up: bfloat16 [64, 768, 4096], P('expert', 'dp'), may hold values from -0.09375 to 0.09375
- w_down: bfloat16 [64, 768, 4096], P('expert', 'dp'), may hold values from -0.21875 to 0.21875
Outputs:
- d_tokens: bfloat16 [6144, 4096], P(('dp', 'expert'))
- d_gate: bfloat16 [64, 768, 4096], P('expert', 'dp')
- d_up: bfloat16 [64, 768, 4096], P('expert', 'dp')
- d_down: bfloat16 [64, 768, 4096], P('expert', 'dp')
Inputs may be any that keep to these rules, and one draw needn't show every extreme that they name: `routes`: each row names 8 different experts. Within the 24 rows of one device no expert is named by more than 4 rows, and in every draw some expert is named by exactly 4 rows of some device.
All inputs are finite; a program needn't handle non-finite values.
Results may differ from a plain program's by a relative error of at most 0.015.
Values may be sent and summed in bfloat16 or wider, within the bound.
A program may use at most 128 MiB of HBM per device.

v0:
```python
from functools import partial

import jax
import jax.numpy as jnp
from jax import lax
from jax.sharding import PartitionSpec as P


def cell_match(routes, experts, capacity):
    expert_ids = jnp.arange(experts, dtype=jnp.int32)
    onehot = (routes[:, :, None] == expert_ids).astype(jnp.int32)
    chosen = jnp.sum(onehot, axis=1)
    earlier = jnp.cumsum(chosen, axis=0) - chosen
    slot_index = jnp.sum(onehot * earlier[:, None, :], axis=2)
    target = routes * capacity + slot_index
    cell_ids = jnp.arange(experts * capacity, dtype=jnp.int32)
    return target[:, :, None] == cell_ids


def placement(matches, experts, capacity):
    return jnp.any(matches, axis=1).reshape(-1, experts, capacity).astype(jnp.bfloat16)


def weighting(matches, gates, experts, capacity):
    spread = jnp.where(matches, gates.astype(jnp.float32)[:, :, None], 0.0)
    return jnp.sum(spread, axis=1).reshape(-1, experts, capacity)


def per_device(tokens, out_grad, routes, gates, w_gate, w_up, w_down):
    tok_rows, features = tokens.shape
    top_count = routes.shape[1]
    experts = lax.axis_size("expert")
    groups = lax.axis_size("dp")
    capacity = max(2, min(tok_rows, 3 * tok_rows * top_count // (2 * experts)))
    match_fn = partial(cell_match, experts=experts, capacity=capacity)
    place_fn = partial(placement, experts=experts, capacity=capacity)
    weight_fn = partial(weighting, experts=experts, capacity=capacity)
    own_match = match_fn(routes)
    own_place = place_fn(own_match)
    own_weight = weight_fn(own_match, gates)
    input_send = jnp.einsum(
        "tec,td->ecd", own_place, tokens, preferred_element_type=jnp.float32
    ).astype(jnp.bfloat16)
    grad_send = jnp.einsum(
        "tec,td->ecd", own_weight, out_grad.astype(jnp.float32), precision=lax.Precision.HIGHEST
    ).astype(jnp.bfloat16)
    input_recv, grad_recv = (
        lax.all_to_all(input_send, "expert", split_axis=0, concat_axis=0, tiled=True),
        lax.all_to_all(grad_send, "expert", split_axis=0, concat_axis=0, tiled=True),
    )
    input_recv = input_recv.reshape(experts, 1, capacity, features)
    grad_recv = grad_recv.reshape(experts, 1, capacity, features)
    input_slots, grad_slots = (
        lax.all_gather(input_recv, "dp", axis=1, tiled=True),
        lax.all_gather(grad_recv, "dp", axis=1, tiled=True),
    )
    input_rows = input_slots.reshape(-1, features)
    grad_rows = grad_slots.reshape(-1, features)
    gate_w = w_gate[0]
    up_w = w_up[0]
    down_w = w_down[0]
    gate_pre = jnp.einsum("rd,fd->rf", input_rows, gate_w, preferred_element_type=jnp.float32)
    up_pre = jnp.einsum("rd,fd->rf", input_rows, up_w, preferred_element_type=jnp.float32)
    sigmoid_gate = jax.nn.sigmoid(gate_pre)
    silu_gate = gate_pre * sigmoid_gate
    hidden = (silu_gate * up_pre).astype(jnp.bfloat16)
    d_hidden = jnp.einsum("rd,fd->rf", grad_rows, down_w, preferred_element_type=jnp.float32)
    d_up_act = (d_hidden * silu_gate).astype(jnp.bfloat16)
    d_gate_act = (
        d_hidden * up_pre * sigmoid_gate * (1.0 + gate_pre * (1.0 - sigmoid_gate))
    ).astype(jnp.bfloat16)
    grad_down = jnp.einsum(
        "rf,rd->fd", hidden, grad_rows, preferred_element_type=jnp.float32
    ).astype(jnp.bfloat16)
    grad_gate = jnp.einsum(
        "rf,rd->fd", d_gate_act, input_rows, preferred_element_type=jnp.float32
    ).astype(jnp.bfloat16)
    grad_up = jnp.einsum(
        "rf,rd->fd", d_up_act, input_rows, preferred_element_type=jnp.float32
    ).astype(jnp.bfloat16)
    partial_sum = jnp.einsum("rf,fd->rd", d_gate_act, gate_w, preferred_element_type=jnp.float32)
    partial_sum = partial_sum + jnp.einsum(
        "rf,fd->rd", d_up_act, up_w, preferred_element_type=jnp.float32
    )
    rounded = partial_sum.astype(jnp.bfloat16).reshape(experts, groups, capacity, features)
    held = lax.optimization_barrier(rounded).astype(jnp.float32)
    slot_total = lax.psum_scatter(
        held.astype(jnp.bfloat16), "dp", scatter_dimension=1, tiled=True
    ).astype(jnp.float32)
    returned = lax.all_to_all(
        slot_total[:, 0].astype(jnp.bfloat16), "expert", split_axis=0, concat_axis=0, tiled=True
    ).astype(jnp.float32)
    summed = jnp.einsum(
        "tec,ecd->td", own_place.astype(jnp.float32), returned, precision=lax.Precision.HIGHEST
    )
    return (summed.astype(jnp.bfloat16), grad_gate[None], grad_up[None], grad_down[None])


def solution(mesh):
    in_specs = (
        P(("dp", "expert"), None),
        P(("dp", "expert"), None),
        P(("dp", "expert"), None),
        P(("dp", "expert"), None),
        P("expert", "dp", None),
        P("expert", "dp", None),
        P("expert", "dp", None),
    )
    out_specs = (
        P(("dp", "expert"), None),
        P("expert", "dp", None),
        P("expert", "dp", None),
        P("expert", "dp", None),
    )
    return jax.shard_map(
        per_device, mesh=mesh, in_specs=in_specs, out_specs=out_specs, check_vma=False
    )
```

profile of v0, /device:TPU:1, one launch (start us, length us, event | category | flops | bytes accessed | tf_op | source)
XLA Modules:
  0.0 475.0 jit_solution(9894178153079241439)
XLA Ops:
  12.5 64.0 %all_to_all.15 = bf16[64,4,4096]{2,1,0:T(4,128)(2,1)S(1)} all-to-all(bf16[64,4,4096]{2,1,0:T(4,128)(2,1)S(1)} %copy.63), channel_id=1, replica_groups=mesh['dp'=4,'expert'=64] {'expert'}, dimensions={0} | all-to-all | bytes 4194304 | tf_op jit(solution)/shard_map/all_to_all | solution.py:48
  76.6 2.5 copy.64
  80.1 1.8 convolution_convert_fusion.1
  83.5 56.9 %all_to_all.16 = bf16[64,4,4096]{2,1,0:T(4,128)(2,1)S(1)} all-to-all(bf16[64,4,4096]{2,1,0:T(4,128)(2,1)S(1)} %copy.59), channel_id=1, replica_groups=mesh['dp'=4,'expert'=64] {'expert'}, dimensions={0} | all-to-all | bytes 4194304 | tf_op jit(solution)/shard_map/all_to_all | solution.py:49
  140.3 2.5 copy.60
  143.1 18.4 %all-gather.7.cloned.1.call-done = bf16[64,16,4096]{2,0,1:T(8,128)(2,1)} async-done(((bf16[64,4,4096]{2,0,1:T(8,128)(2,1)}), bf16[64,16,4096]{2,0,1:T(8,128)(2,1)}) %all-gather.7.cloned.1.call-update) | async-done | bytes 8388624 | tf_op jit(solution)/shard_map/all_gather | solution.py:54
  161.5 11.2 %copy.65 = bf16[64,16,4096]{2,1,0:T(8,128)(2,1)} copy(bf16[64,16,4096]{2,0,1:T(8,128)(2,1)} %all-gather.7.cloned.1.call-done) | data formatting | bytes 16777216 | tf_op jit(solution)/shard_map/all_gather | solution.py:54
  172.8 7.5 %fusion.7 = f32[1024,192]{0,1:T(8,128)} fusion(bf16[1024,4096]{1,0:T(8,128)(2,1)} %bitcast.48, bf16[1,192,4096]{2,1,0:T(8,128)(2,1)S(1)} %copy-done), kind=kOutput, calls=%fused_computation.14 | convolution fusion | flops 1610612736 | bytes 10747904 | tf_op jit(solution)/shard_map/rd,fd->rf/dot_general | solution.py:62
  180.3 3.8 fusion.10
  184.2 65.9 %all-gather.5.cloned.1.call-done = bf16[64,16,4096]{2,0,1:T(8,128)(2,1)} async-done(((bf16[64,4,4096]{2,0,1:T(8,128)(2,1)}), bf16[64,16,4096]{2,0,1:T(8,128)(2,1)}) %all-gather.5.cloned.1.call-update) | async-done | bytes 8388624 | tf_op jit(solution)/shard_map/all_gather | solution.py:55
  250.1 11.6 %copy.61 = bf16[64,16,4096]{2,1,0:T(8,128)(2,1)} copy(bf16[64,16,4096]{2,0,1:T(8,128)(2,1)} %all-gather.5.cloned.1.call-done) | data formatting | bytes 16777216 | tf_op jit(solution)/shard_map/all_gather | solution.py:55
  261.6 6.4 %multiply_convert_fusion.1 = (bf16[1024,192]{0,1:T(8,128)(2,1)S(1)}, bf16[1024,192]{0,1:T(8,128)(2,1)S(1)}) fusion(f32[1024,192]{0,1:T(8,128)S(1)} %copy-done.9, f32[1024,192]{0,1:T(8,128)S(1)} %copy-done.11, bf16[1024,4096]{1,0:T(8,128)(2,1)} %bitcast.52, bf16[1,192,4096]{2,1,0:T(8,128)(2,1)S(1)} %copy-done.8), kind=kOutput, calls=%fused_computation.22 | convolution fusion | flops 1613168640 | bytes 12320768 | tf_op jit(solution)/shard_map/rd,fd->rf/dot_general | solution.py:67
  268.1 8.1 %fusion.5 = f32[1024,4096]{1,0:T(8,128)} fusion(bf16[1024,192]{0,1:T(8,128)(2,1)S(1)} %get-tuple-element.5, bf16[1,192,4096]{2,1,0:T(8,128)(2,1)S(1)} %copy-done), kind=kOutput, calls=%fused_computation.12 | convolution fusion | flops 1610612736 | bytes 18743296 | tf_op jit(solution)/shard_map/rf,fd->rd/dot_general | solution.py:81
  276.2 11.4 %add_convert_fusion = bf16[1024,4096]{1,0:T(8,128)(2,1)} fusion(f32[1024,4096]{1,0:T(8,128)} %fusion.5, bf16[1024,192]{0,1:T(8,128)(2,1)S(1)} %get-tuple-element.4, bf16[1,192,4096]{2,1,0:T(8,128)(2,1)S(1)} %copy-done.3), kind=kOutput, calls=%fused_computation | convolution fusion | flops 1619001344 | bytes 27131904 | tf_op jit(solution)/shard_map/rf,fd->rd/dot_general | solution.py:82
  287.6 13.3 %reshape.48 = bf16[64,4,4,4096]{3,2,1,0:T(4,128)(2,1)} reshape(bf16[1024,4096]{1,0:T(8,128)(2,1)} %add_convert_fusion) | data formatting | bytes 16777216 | tf_op jit(solution)/shard_map/reshape | solution.py:85
  300.9 11.2 %copy.66 = bf16[64,4,4,4096]{3,0,2,1:T(8,128)(2,1)} copy(bf16[64,4,4,4096]{3,2,1,0:T(4,128)(2,1)} %reshape.48) | data formatting | bytes 16777216 | tf_op jit(solution)/shard_map/optimization_barrier | solution.py:86
  312.1 84.3 %reduce-scatter.2.cloned.1.call-done = bf16[64,1,4,4096]{3,0,2,1:T(8,128)(2,1)} async-done(((bf16[64,4,4,4096]{3,0,2,1:T(8,128)(2,1)}), bf16[64,1,4,4096]{3,0,2,1:T(8,128)(2,1)}) %reduce-scatter.2.cloned.1.call-update) | async-done | bytes 2097168 | tf_op jit(solution)/shard_map/reduce_scatter | solution.py:87
  396.4 4.6 copy.67
  401.0 11.4 %all-to-all-start.2 = ((bf16[64,4,4096]{2,1,0:T(4,128)(2,1)}), bf16[64,4,4096]{2,1,0:T(4,128)(2,1)}, u32[]{:S(2)}, u32[]{:S(2)}) async-start(bf16[64,4,4096]{2,1,0:T(4,128)(2,1)} %copy.67), calls=%async_computation.3 | async-start | bytes 4194304 | tf_op jit(solution)/shard_map/all_to_all | solution.py:90
  412.4 6.3 %fusion.1 = bf16[1,192,4096]{2,1,0:T(8,128)(2,1)} fusion(bf16[1024,192]{0,1:T(8,128)(2,1)S(1)} %copy-done.5, bf16[1024,4096]{1,0:T(8,128)(2,1)} %bitcast.49), kind=kOutput, calls=%fused_computation.7 | convolution fusion | flops 1611399168 | bytes 10354688 | tf_op jit(solution)/shard_map/rf,rd->fd/dot_general | solution.py:78
  418.7 6.4 %fusion = bf16[1,192,4096]{2,1,0:T(8,128)(2,1)} fusion(bf16[1024,192]{0,1:T(8,128)(2,1)S(1)} %get-tuple-element.5, bf16[1024,4096]{1,0:T(8,128)(2,1)} %bitcast.50), kind=kOutput, calls=%fused_computation.6 | convolution fusion | flops 1611399168 | bytes 10354688 | tf_op jit(solution)/shard_map/rf,rd->fd/dot_general | solution.py:75
  425.2 6.5 %fusion.2 = bf16[1,192,4096]{2,1,0:T(8,128)(2,1)} fusion(bf16[1024,4096]{1,0:T(8,128)(2,1)} %bitcast.53, f32[1024,192]{0,1:T(8,128)S(1)} %copy-done.12, f32[1024,192]{0,1:T(8,128)S(1)} %copy-done.10), kind=kOutput, calls=%fused_computation.8 | convolution fusion | flops 1612578816 | bytes 11534336 | tf_op jit(solution)/shard_map/rf,rd->fd/dot_general | solution.py:72
  431.7 31.7 %all-to-all-done.2 = bf16[64,4,4096]{2,1,0:T(4,128)(2,1)} async-done(((bf16[64,4,4096]{2,1,0:T(4,128)(2,1)}), bf16[64,4,4096]{2,1,0:T(4,128)(2,1)}, u32[]{:S(2)}, u32[]{:S(2)}) %all-to-all-start.2) | async-done | bytes 2097184 | tf_op jit(solution)/shard_map/all_to_all | solution.py:90
  463.4 4.6 fusion.3
  (47 shorter events, 8.2 us)
Async XLA Ops:
  7.2 165.6 %copy-start = (bf16[1,192,4096]{2,1,0:T(8,128)(2,1)S(1)}, bf16[1,192,4096]{2,1,0:T(8,128)(2,1)}, u32[]{:S(2)}) copy-start(bf16[1,192,4096]{2,1,0:T(8,128)(2,1)} %param.11) | copy-start | bytes 4718596
  7.2 154.4 %all-gather.7.cloned.1.call-start = ((), (), s32[]{:S(2)}) async-start(), calls=%async_computation.6 | async-start | bytes 10485760 | tf_op jit(solution)/shard_map/all_gather | solution.py:54
  79.1 0.7 copy-start.7
  79.1 1.0 copy-start.6
  79.1 171.0 %all-gather.5.cloned.1.call-start = ((), (), s32[]{:S(2)}) async-start(), calls=%async_computation.5 | async-start | bytes 10485760 | tf_op jit(solution)/shard_map/all_gather | solution.py:55
  142.9 253.6 %reduce-scatter.2.cloned.1.call-start = ((), (), s32[]{:S(2)}) async-start(), calls=%async_computation.4 | async-start | bytes 10485760 | tf_op jit(solution)/shard_map/reduce_scatter | solution.py:87
  172.8 7.5 %copy-start.2 = (bf16[64,16,4096]{2,1,0:T(8,128)(2,1)S(1)}, bf16[64,16,4096]{2,1,0:T(8,128)(2,1)}, u32[]{:S(2)}) copy-start(bf16[64,16,4096]{2,1,0:T(8,128)(2,1)} %copy.65) | copy-start | bytes 25165828
  172.8 7.6 %copy-start.3 = (bf16[1,192,4096]{2,1,0:T(8,128)(2,1)S(1)}, bf16[1,192,4096]{2,1,0:T(8,128)(2,1)}, u32[]{:S(2)}) copy-start(bf16[1,192,4096]{2,1,0:T(8,128)(2,1)} %param.12) | copy-start | bytes 4718596
  250.1 11.6 %copy-start.8 = (bf16[1,192,4096]{2,1,0:T(8,128)(2,1)S(1)}, bf16[1,192,4096]{2,1,0:T(8,128)(2,1)}, u32[]{:S(2)}) copy-start(bf16[1,192,4096]{2,1,0:T(8,128)(2,1)} %param.13) | copy-start | bytes 4718596
  250.1 11.6 %copy-start.9 = (f32[1024,192]{0,1:T(8,128)S(1)}, f32[1024,192]{0,1:T(8,128)}, u32[]{:S(2)}) copy-start(f32[1024,192]{0,1:T(8,128)} %fusion.7) | copy-start | bytes 2359300
  250.1 11.6 %copy-start.11 = (f32[1024,192]{0,1:T(8,128)S(1)}, f32[1024,192]{0,1:T(8,128)}, u32[]{:S(2)}) copy-start(f32[1024,192]{0,1:T(8,128)} %fusion.10) | copy-start | bytes 2359300
  268.1 8.1 %copy-start.4 = (bf16[1024,192]{0,1:T(8,128)(2,1)}, bf16[1024,192]{0,1:T(8,128)(2,1)S(1)}, u32[]{:S(2)}) copy-start(bf16[1024,192]{0,1:T(8,128)(2,1)S(1)} %get-tuple-element.4) | copy-start | bytes 1179652
  401.0 11.4 %copy-start.5 = (bf16[1024,192]{0,1:T(8,128)(2,1)S(1)}, bf16[1024,192]{0,1:T(8,128)(2,1)}, u32[]{:S(2)}) copy-start(bf16[1024,192]{0,1:T(8,128)(2,1)} %copy-done.4) | copy-start | bytes 1179652
  401.0 62.4 %all-to-all-start.2 = ((bf16[64,4,4096]{2,1,0:T(4,128)(2,1)}), bf16[64,4,4096]{2,1,0:T(4,128)(2,1)}, u32[]{:S(2)}, u32[]{:S(2)}) async-start(bf16[64,4,4096]{2,1,0:T(4,128)(2,1)} %copy.67), calls=%async_computation.3 | async-start | bytes 4194304 | tf_op jit(solution)/shard_map/all_to_all | solution.py:90
  418.7 6.5 %copy-start.10 = (f32[1024,192]{0,1:T(8,128)S(1)}, f32[1024,192]{0,1:T(8,128)}, u32[]{:S(2)}) copy-start(f32[1024,192]{0,1:T(8,128)} %fusion.7) | copy-start | bytes 2359300
  418.7 6.5 %copy-start.12 = (f32[1024,192]{0,1:T(8,128)S(1)}, f32[1024,192]{0,1:T(8,128)}, u32[]{:S(2)}) copy-start(f32[1024,192]{0,1:T(8,128)} %fusion.10) | copy-start | bytes 2359300
  425.2 42.8 %copy-start.1 = (bf16[1,192,4096]{2,1,0:T(8,128)(2,1)S(1)}, bf16[1,192,4096]{2,1,0:T(8,128)(2,1)}, u32[]{:S(2)}) copy-start(bf16[1,192,4096]{2,1,0:T(8,128)(2,1)} %param.11) | copy-start | bytes 4718596
Sparse Core Ops, SparseCore 0:
  79.2 82.2 all-gather.6
  163.4 86.6 all-gather.4
  312.3 84.1 reduce-scatter.1
where the time goes:
time: 484 us; the launch traced here: 475 us
  waiting for transfers between devices  200 us (41%)
  blocking collectives  121 us (25%)
  matrix products  64.6 us (13%)
  local copies, waits for them, and re-layouts  62.1 us (13%)
  between operations  14.4 us (3%)
  starting transfers between devices  11.7 us (2%)
    reduce_scatter x1, waiting for transfers between devices, per_device(): lax.psum_scatter(held.astype(jnp.bfloat16), 'dp', scatter_dimension=1, ti...  84.3 us
    all_gather x1, waiting for transfers between devices, per_device(): lax.all_gather(grad_recv, 'dp', axis=1, tiled=True)  65.9 us
    all_to_all x1, blocking collectives, per_device(): lax.all_to_all(input_send, 'expert', split_axis=0, concat_axis=0, tiled=T...  64 us
    all_to_all x1, blocking collectives, per_device(): lax.all_to_all(grad_send, 'expert', split_axis=0, concat_axis=0, tiled=True)  56.9 us
    all_to_all x1, waiting for transfers between devices, per_device(): lax.all_to_all(slot_total[:, 0].astype(jnp.bfloat16), 'expert', split_axi...  31.7 us
    all_gather x1, waiting for transfers between devices, per_device(): lax.all_gather(input_recv, 'dp', axis=1, tiled=True)  18.4 us
    reshape x1, local copies, waits for them, and re-layouts, per_device(): partial_sum.astype(jnp.bfloat16)  13.3 us
    all_gather x1, local copies, waits for them, and re-layouts, per_device(): lax.all_gather(grad_recv, 'dp', axis=1, tiled=True)  11.6 us
  transfers between devices with their start and end apart: 4, of which 4 were waited for; matrix products, arithmetic and copies ran while one was open for 10% of the time, Pallas kernels for 0%

commit v1 on v0

v1 whole, which is shorter than its diff:
```python
import jax
import jax.numpy as jnp
from jax import lax
from jax.experimental import pallas as pl
from jax.experimental.pallas import tpu as pltpu
from jax.sharding import PartitionSpec as P

MESH = pl.DeviceIdType.MESH
F32, BF16 = jnp.float32, jnp.bfloat16
VMEM_LIMIT = 67043328

NY, NX, NZ, NCORE = 4, 4, 8, 2
CAP = 4
TOK = 24
PAD = 32
SRC = NX * NCORE
ROWS = NZ * CAP


class Place:
    def __init__(self):
        self.y = lax.axis_index("dp")
        e = lax.axis_index("expert")
        self.c = lax.rem(e, NCORE)
        self.z = lax.rem(lax.div(e, NCORE), NZ)
        self.x = lax.div(e, NCORE * NZ)

    @staticmethod
    def first(i):
        return i + 1 - 2 * lax.rem(i, 2)

    @staticmethod
    def second(i):
        return 3 - i

    def pick(self, i, s):
        return (1 - s) * self.first(i) + s * self.second(i)

    def at(self, y=None, x=None, z=None, c=None):
        y = self.y if y is None else y
        x = self.x if x is None else x
        z = self.z if z is None else z
        c = self.c if c is None else c
        return (y, (x * NZ + z) * NCORE + c)

    def zz(self, d):
        return lax.rem(self.z + d + NZ, NZ)

    def enter(self):
        sem = pltpu.get_barrier_semaphore()
        peers = [self.at(y=self.first(self.y)), self.at(y=self.second(self.y))]
        peers += [self.at(z=self.zz(1)), self.at(z=self.zz(-1)), self.at(c=1 - self.c)]
        for x in (self.first(self.x), self.second(self.x)):
            peers += [self.at(x=x, c=0), self.at(x=x, c=1)]
        for p in peers:
            pl.semaphore_signal(sem, inc=1, device_id=p, device_id_type=MESH)
        pl.semaphore_wait(sem, len(peers))


def send(src, dst, ssem, rsem, device):
    pltpu.make_async_remote_copy(
        src_ref=src, dst_ref=dst, send_sem=ssem, recv_sem=rsem, device_id=device, device_id_type=MESH
    ).start()


def await_(ref, sem):
    pltpu.make_async_copy(ref, ref, sem).wait()


def when(i, n):
    return pl.when(jnp.logical_and(i >= 0, i < n))


def dot(a, b, dims=((1,), (0,))):
    return lax.dot_general(a, b, (dims, ((), ())), preferred_element_type=F32)


def slot_exchange(p, s, i, sel, fwd, into, send_sem, fwd_send, fwd_recv, recv_sem):
    mine = p.c
    send(sel.at[i, :, 1 - mine], into.at[:, mine], send_sem, recv_sem, p.at(c=1 - mine))
    send(sel.at[i, :, pl.ds(6, 2)], fwd.at[i], send_sem, fwd_recv, p.at(x=p.pick(p.x, s)))
    for d, x in ((1, p.first(p.x)), (2, p.second(p.x))):
        for c in range(NCORE):
            send(sel.at[i, :, d * 2 + c], into.at[:, d * 2 + mine], send_sem, recv_sem, p.at(x=x, c=c))


def pass_on(p, s, i, fwd, into, fwd_send, recv_sem):
    for c in range(NCORE):
        send(fwd.at[i, :, c], into.at[:, 6 + p.c], fwd_send, recv_sem, p.at(x=p.pick(p.x, 1 - s), c=c))


def quarter(pos, s):
    return (0, 1 + s, 2 - s, 3)[pos]


def route_stage(tok, info, wg, wu, wd, rows_out, act_t_out, act_out, st_out,
                zbuf, sel, fwd, rows, wgu, wdn, acc_gu, acc_d, sm, rb,
                sem_l, a_s, a_r, z_s, z_r, x_s, x_r, f_s, f_r, l_s, l_r, o_s, r_s, r_r):
    p = Place()
    n, _, w = tok.shape
    half = n // 2
    hid = wg.shape[0]
    y1, y2 = p.first(p.y), p.second(p.y)

    own_tok = pltpu.make_async_copy(tok, zbuf.at[:, 0, p.z], sem_l.at[0])
    own_tok.start()
    own_info = pltpu.make_async_copy(info, rb.at[0, p.z], sem_l.at[1])
    own_info.start()
    loads = [
        pltpu.make_async_copy(wg, wgu.at[pl.ds(0, hid)], sem_l.at[2]),
        pltpu.make_async_copy(wu, wgu.at[pl.ds(hid, hid)], sem_l.at[3]),
        pltpu.make_async_copy(wd, wdn, sem_l.at[4]),
    ]
    for cp in loads:
        cp.start()
    p.enter()
    send(info, rb.at[1, p.z], r_s.at[7], r_r.at[7], p.at(y=y1))
    send(info, rb.at[2, p.z], r_s.at[8], r_r.at[8], p.at(y=y2))

    @pl.loop(0, n)
    def _(i):
        send(tok.at[i], zbuf.at[i, 1, p.z], a_s.at[i], a_r.at[i], p.at(y=p.pick(p.y, lax.rem(i, 2))))

    acc_gu[...] = jnp.zeros_like(acc_gu)
    acc_d[...] = jnp.zeros_like(acc_d)

    def z_hop(buf, k, ssem, rsem):
        for side, d in ((0, 1), (1, -1)):
            block = p.zz(-d * (k - 1))
            send(buf.at[:, block], buf.at[:, block], ssem(2 * (k - 1) + side), rsem.at[2 * (k - 1) + side], p.at(z=p.zz(d)))

    def z_last(buf, s, ssem, rsem):
        d = 1 - 2 * s
        block = p.zz(-3 * d)
        send(buf.at[:, block], buf.at[:, block], ssem(6), rsem.at[6], p.at(z=p.zz(d)))

    def z_wait(buf, k, rsem):
        for side in (0, 1):
            await_(buf.at[:, 0], rsem.at[2 * (k - 1) + side])

    def info_step(t):
        one = lambda j: r_s.at[j]

        @pl.when(t == 0)
        def _():
            own_info.wait()
            await_(info, r_r.at[7])
            await_(info, r_r.at[8])
            z_hop(rb, 1, one, r_r)

        for k in (1, 2):

            @pl.when(t == k)
            def _(k=k):
                z_wait(rb, k, r_r)
                z_hop(rb, k + 1, one, r_r)

        @pl.when(t == 3)
        def _():
            z_wait(rb, 3, r_r)
            z_last(rb, 0, one, r_r)

        @pl.when(t == 4)
        def _():
            await_(rb.at[:, 0], r_r.at[6])
            select_matrices()

    def select_matrices():
        lane = lax.broadcasted_iota(jnp.int32, (128, 128), 1)
        sub = lax.broadcasted_iota(jnp.int32, (128, 128), 0)
        before = jnp.where(jnp.logical_and(sub < lane, lax.div(sub, PAD) == lax.div(lane, PAD)), 1.0, 0.0).astype(BF16)
        r_row = lax.broadcasted_iota(jnp.int32, (ROWS, 128), 0)
        r_lane = lax.broadcasted_iota(jnp.int32, (ROWS, 128), 1)
        row_z, row_slot = lax.div(r_row, CAP), lax.rem(r_row, CAP).astype(F32)
        xs = (p.x, p.first(p.x), p.second(p.x), lax.rem(p.x + 2, NX))
        for role in range(3):
            for zh in range(2):
                both = rb[role, 4 * zh].astype(F32)
                for q in range(1, 4):
                    both = both + rb[role, 4 * zh + q].astype(F32)
                route, gate = both[0:8].astype(jnp.int32), both[8:16]
                chosen, value = [], []
                for d in range(4):
                    for c in range(NCORE):
                        hit = route == (xs[d] * NZ + p.z) * NCORE + c + 1
                        chosen.append(jnp.sum(jnp.where(hit, 1.0, 0.0), axis=0, keepdims=True))
                        value.append(jnp.sum(jnp.where(hit, gate, 0.0), axis=0, keepdims=True))
                chosen = jnp.concatenate(chosen, axis=0)
                earlier = dot(chosen.astype(BF16), before)
                same_z = row_z == 4 * zh + lax.div(r_lane, PAD)
                for e in range(SRC):
                    spread = lambda v: jnp.broadcast_to(v, (ROWS, 128))
                    hit = jnp.logical_and(same_z, jnp.logical_and(spread(chosen[e : e + 1]) > 0.5, spread(earlier[e : e + 1]) == row_slot))
                    place = (pl.ds(e * ROWS, ROWS), pl.ds(zh * 128, 128))
                    sm[0, role, place[0], place[1]] = jnp.where(hit, 1.0, 0.0).astype(BF16)
                    sm[1, role, place[0], place[1]] = jnp.where(hit, spread(value[e]), 0.0).astype(BF16)
            st_out[role] = sm[0, role].astype(F32).T.astype(BF16)

    def step(t, carry):
        i6, i5, i4, i3, i2, i1 = (t - k for k in (6, 5, 4, 3, 2, 1))

        @when(i6, n)
        def _():
            await_(rows.at[i6, 0, :, pl.ds(0, 7)], x_r.at[i6])
            late = p.at(y=p.pick(p.y, 1 - lax.rem(i6, 2)))
            send(rows.at[i6, 0], rows.at[i6, 1], l_s.at[i6], l_r.at[i6], late)

        @when(i5, n)
        def _():
            await_(fwd.at[i5], f_r.at[i5])
            pass_on(p, lax.rem(i5, 2), i5, fwd, rows.at[i5, 0], f_s.at[i5], x_r.at[i5])

        info_step(t)

        @when(i4, n)
        def _():
            s = lax.rem(i4, 2)
            which = lax.div(i4, half)
            await_(zbuf.at[i4, :, 0], z_r.at[i4, 6])
            for ys, role in ((0, 0), (1, 1 + s)):
                got = dot(sm[which, role], zbuf[i4, ys].reshape(NZ * PAD, w)).astype(BF16)
                sel[i4, ys] = got.reshape(SRC, ROWS, w)
            rows[i4, 0, :, p.c] = sel[i4, :, p.c]
            slot_exchange(p, s, i4, sel, fwd, rows.at[i4, 0], x_s.at[i4], f_s.at[i4], f_r.at[i4], x_r.at[i4])

        @when(i3, n)
        def _():
            z_wait(zbuf.at[i3], 3, z_r.at[i3])
            z_last(zbuf.at[i3], lax.rem(i3, 2), lambda j: z_s.at[i3], z_r.at[i3])

        for i, k in ((i2, 2), (i1, 1)):

            @when(i, n)
            def _(i=i, k=k):
                z_wait(zbuf.at[i], k, z_r.at[i])
                z_hop(zbuf.at[i], k + 1, lambda j: z_s.at[i], z_r.at[i])

        @when(t, n)
        def _():
            @pl.when(t == 0)
            def _():
                own_tok.wait()

            await_(tok.at[t], a_r.at[t])
            z_hop(zbuf.at[t], 1, lambda j: z_s.at[t], z_r.at[t])

        i8 = t - 8

        @pl.when(i8 == 0)
        def _():
            for cp in loads:
                cp.wait()

        @when(i8, n)
        def _():
            s = lax.rem(i8, 2)
            await_(rows.at[i8, 1], l_r.at[i8])
            for h in range(2):
                for ys in range(2):
                    k = pl.multiple_of((2 * h + ys) * SRC * ROWS, SRC * ROWS)
                    pltpu.make_async_copy(rows.at[i8, h, ys], rows_out.at[i8, 2 * h + ys], o_s.at[i8, 2 * h + ys]).start()

            def multiply(acc, weights):
                j = lax.rem(i8, half)
                cols = weights[:, pl.ds(pl.multiple_of(j * w, w), w)]
                for h in range(2):
                    for ys in range(2):
                        q = quarter(2 * h + ys, s)
                        at = pl.ds(pl.multiple_of(q * SRC * ROWS, SRC * ROWS), SRC * ROWS)
                        acc[:, at] += dot(cols, rows[i8, h, ys].reshape(SRC * ROWS, w), ((1,), (1,)))

            @pl.when(i8 < half)
            def _():
                multiply(acc_gu, wgu)

            @pl.when(i8 >= half)
            def _():
                multiply(acc_d, wdn)

        return carry

    lax.fori_loop(0, n + 8, step, 0)

    for q in range(4):
        at = pl.ds(q * SRC * ROWS, SRC * ROWS)
        gate_pre, up_pre, d_hidden = acc_gu[0:hid, at], acc_gu[hid : 2 * hid, at], acc_d[:, at]
        sig = jax.nn.sigmoid(gate_pre)
        silu = gate_pre * sig
        d_up = d_hidden * silu
        d_gate = d_hidden * up_pre * sig * (1.0 + gate_pre * (1.0 - sig))
        both = jnp.concatenate([d_gate, d_up], axis=0)
        act_t_out[0 : 2 * hid, at] = both.astype(BF16)
        act_t_out[2 * hid : 3 * hid, at] = (silu * up_pre).astype(BF16)
        act_out[at, :] = both.T.astype(BF16)

    @pl.loop(0, n)
    def _(i):
        await_(tok.at[i], a_s.at[i])
        await_(zbuf.at[i, :, pl.ds(0, 7)], z_s.at[i])
        await_(sel.at[i, :, pl.ds(0, 7)], x_s.at[i])
        await_(fwd.at[i], f_s.at[i])
        await_(rows.at[i, 0], l_s.at[i])
        for k in range(4):
            await_(rows.at[i, 0, 0], o_s.at[i, k])

    for j in range(7):
        await_(rb.at[:, 0], r_s.at[j])
    await_(info, r_s.at[7])
    await_(info, r_s.at[8])


def return_stage(act, act_t, st, wg, wu, rows_in, d_tok, d_gate, d_up, d_down,
                 wgu, acts, keep, part, got, total, fwd, back, own, zs, zr, tail, tail_in, xr, gr, dw_gu, dw_d,
                 sem_l, in_s, l_s, l_r, x_s, x_r, f_s, f_r, z_s, z_r, e_s, e_r, o_s):
    p = Place()
    n, w = keep.shape[0], keep.shape[-1]
    hid = wg.shape[0]
    qr = SRC * ROWS

    loads = [
        pltpu.make_async_copy(wg, wgu.at[pl.ds(0, hid)], sem_l.at[0]),
        pltpu.make_async_copy(wu, wgu.at[pl.ds(hid, hid)], sem_l.at[1]),
    ]
    for cp in loads:
        cp.start()

    def fetch(i, slot):
        pltpu.make_async_copy(rows_in.at[i], xr.at[slot], in_s.at[slot, 0]).start()
        pltpu.make_async_copy(rows_in.at[n + i], gr.at[slot], in_s.at[slot, 1]).start()

    fetch(0, 0)
    p.enter()
    acts[0] = act_t[...]
    for pos in range(4):
        acts[1, :, pl.ds(pos * qr, qr)] = act_t[:, pl.ds(quarter(pos, 1) * qr, qr)]
    for cp in loads:
        cp.wait()

    def z_send(i, k, side, src):
        j = 6 if k == 4 else 2 * (k - 1) + side
        d = 2 * side - 1
        send(src, zr.at[i, j], z_s.at[i, j], z_r.at[i, j], p.at(z=p.zz(d)))

    def step(t, carry):
        i1, i2, i3, i4, i5, i6, i7, i8 = (t - k for k in range(1, 9))

        @when(t, n)
        def _():
            s = lax.rem(t, 2)
            cols = wgu[:, pl.ds(pl.multiple_of(t * w, w), w)]
            for pos in (2, 3, 0, 1):
                q = quarter(pos, s)
                a = act[pl.ds(pl.multiple_of(q * qr, qr), qr), :]
                value = dot(a, cols).astype(BF16).reshape(SRC, ROWS, w)
                if pos >= 2:
                    part[t, pos - 2] = value
                else:
                    keep[t, pos] = value
                if pos == 3:
                    late = p.at(y=p.pick(p.y, 1 - s))
                    send(part.at[t], got.at[t], l_s.at[t], l_r.at[t], late)

        @when(i1, n)
        def _():
            s = lax.rem(i1, 2)
            await_(got.at[i1], l_r.at[i1])
            total[i1] = (keep[i1].astype(F32) + got[i1].astype(F32)).astype(BF16)
            back[i1, :, p.c] = total[i1, :, p.c]
            slot_exchange(p, s, i1, total, fwd, back.at[i1], x_s.at[i1], f_s.at[i1], f_r.at[i1], x_r.at[i1])

        @when(i2, n)
        def _():
            await_(fwd.at[i2], f_r.at[i2])
            pass_on(p, lax.rem(i2, 2), i2, fwd, back.at[i2], f_s.at[i2], x_r.at[i2])

        @when(i3, n)
        def _():
            s = lax.rem(i3, 2)
            await_(back.at[i3, :, pl.ds(0, 7)], x_r.at[i3])
            for ys, role in ((0, 0), (1, 1 + s)):
                value = dot(st[role], back[i3, ys].reshape(qr, w)).astype(BF16)
                own[i3, ys] = value.reshape(NZ, PAD, w)
            block = own.at[i3, :, p.zz(4)]
            d = 2 * s - 1
            send(block, zr.at[i3, 6], z_s.at[i3, 6], z_r.at[i3, 6], p.at(z=p.zz(d)))

        @when(i4, n)
        def _():
            s = lax.rem(i4, 2)
            await_(zr.at[i4, 6], z_r.at[i4, 6])
            four = zr[i4, 6].astype(F32)
            for side in (0, 1):
                mine = own[i4, :, p.zz(3 * (2 * side - 1))].astype(F32)
                add = four * jnp.where(s == side, 1.0, 0.0)
                zs[i4, 4 + side] = (mine + add).astype(BF16)
                z_send(i4, 3, side, zs.at[i4, 4 + side])

        for i, k in ((i5, 2), (i6, 1)):

            @when(i, n)
            def _(i=i, k=k):
                for side in (0, 1):
                    await_(zr.at[i, 0], z_r.at[i, 2 * k + side])
                    mine = own[i, :, p.zz(k * (2 * side - 1))].astype(F32)
                    j = 2 * (k - 1) + side
                    zs[i, j] = (mine + zr[i, 2 * k + side].astype(F32)).astype(BF16)
                    z_send(i, k, side, zs.at[i, j])

        @when(i7, n)
        def _():
            for side in (0, 1):
                await_(zr.at[i7, 0], z_r.at[i7, side])
            value = own[i7, :, p.z].astype(F32) + zr[i7, 0].astype(F32) + zr[i7, 1].astype(F32)
            zs[i7, 6, 0] = value[0].astype(BF16)
            tail[i7] = value[1].astype(BF16)
            send(tail.at[i7], tail_in.at[i7], e_s.at[i7], e_r.at[i7], p.at(y=p.pick(p.y, lax.rem(i7, 2))))

        @when(i8, n)
        def _():
            await_(tail_in.at[i8], e_r.at[i8])
            value = zs[i8, 6, 0].astype(F32) + tail_in[i8].astype(F32)
            d_tok[:, pl.ds(pl.multiple_of(i8 * w, w), w)] = value[0:TOK].astype(BF16)

        @when(t, n)
        def _():
            slot = lax.rem(t, 2)

            @pl.when(t + 1 < n)
            def _():
                fetch(t + 1, 1 - slot)

            await_(xr.at[slot], in_s.at[slot, 0])
            await_(gr.at[slot], in_s.at[slot, 1])
            a = acts[slot]
            x_all = xr[slot].reshape(4 * qr, w)
            g_all = gr[slot].reshape(4 * qr, w)
            dw_gu[t] = dot(a[0 : 2 * hid], x_all).astype(BF16)
            dw_d[t] = dot(a[2 * hid : 3 * hid], g_all).astype(BF16)
            at = pl.ds(pl.multiple_of(t * w, w), w)
            pltpu.make_async_copy(dw_gu.at[t, pl.ds(0, hid)], d_gate.at[:, at], o_s.at[t, 0]).start()
            pltpu.make_async_copy(dw_gu.at[t, pl.ds(hid, hid)], d_up.at[:, at], o_s.at[t, 1]).start()
            pltpu.make_async_copy(dw_d.at[t], d_down.at[:, at], o_s.at[t, 2]).start()

        return carry

    lax.fori_loop(0, n + 8, step, 0)

    @pl.loop(0, n)
    def _(i):
        await_(part.at[i], l_s.at[i])
        await_(total.at[i, :, pl.ds(0, 7)], x_s.at[i])
        await_(fwd.at[i], f_s.at[i])
        for j in range(7):
            await_(zr.at[i, j], z_s.at[i, j])
        await_(tail.at[i], e_s.at[i])
        for j in range(3):
            await_(dw_d.at[i], o_s.at[i, j])


def per_device(tokens, out_grad, routes, gates, w_gate, w_up, w_down):
    width = tokens.shape[1]
    w = 512
    nc = width // w
    n = 2 * nc
    hid = w_gate.shape[1]
    qr = SRC * ROWS
    z = lax.rem(lax.div(lax.axis_index("expert"), NCORE), NZ)

    def chunks(a):
        a = jnp.pad(a, ((0, PAD - TOK), (0, 0)))
        return a.reshape(PAD, nc, w).transpose(1, 0, 2)

    tok = jnp.concatenate([chunks(tokens), chunks(out_grad)], axis=0)
    info = jnp.concatenate([(routes + 1).astype(BF16).T, gates.T], axis=0)
    info = jnp.pad(info, ((0, 0), (0, PAD - TOK)))
    info = jnp.where(lax.broadcasted_iota(jnp.int32, (16, 4, PAD), 1) == lax.rem(z, 4), info[:, None, :], 0).reshape(16, 128)

    anywhere = pl.BlockSpec(memory_space=pl.ANY)
    vmem = pl.BlockSpec(memory_space=pltpu.VMEM)
    dma = pltpu.SemaphoreType.DMA
    shape = jax.ShapeDtypeStruct
    rows, act_t, act, st = pl.pallas_call(
        route_stage,
        out_shape=(shape((n, 4, SRC, ROWS, w), BF16), shape((3 * hid, 4 * qr), BF16), shape((4 * qr, 2 * hid), BF16), shape((3, qr, qr), BF16)),
        in_specs=[anywhere, vmem, anywhere, anywhere, anywhere],
        out_specs=(anywhere, vmem, vmem, vmem),
        scratch_shapes=[
            pltpu.VMEM((n, 2, NZ, PAD, w), BF16),
            pltpu.VMEM((n, 2, SRC, ROWS, w), BF16),
            pltpu.VMEM((n, 2, 2, ROWS, w), BF16),
            pltpu.VMEM((n, 2, 2, SRC, ROWS, w), BF16),
            pltpu.VMEM((2 * hid, width), BF16),
            pltpu.VMEM((hid, width), BF16),
            pltpu.VMEM((2 * hid, 4 * qr), F32),
            pltpu.VMEM((hid, 4 * qr), F32),
            pltpu.VMEM((2, 3, qr, qr), BF16),
            pltpu.VMEM((3, NZ, 16, 128), BF16),
            dma((5,)), dma((n,)), dma((n,)), dma((n,)), dma((n, 7)), dma((n,)), dma((n,)), dma((n,)), dma((n,)),
            dma((n,)), dma((n,)), dma((n, 4)), dma((9,)), dma((9,)),
        ],
        compiler_params=pltpu.CompilerParams(collective_id=0, has_side_effects=True, vmem_limit_bytes=VMEM_LIMIT),
    )(tok, info, w_gate[0], w_up[0], w_down[0])

    n = nc
    d_tok, d_gate, d_up, d_down = pl.pallas_call(
        return_stage,
        out_shape=(shape((TOK, width), BF16),) + (shape((hid, width), BF16),) * 3,
        in_specs=[vmem, vmem, vmem, anywhere, anywhere, anywhere],
        out_specs=(vmem, anywhere, anywhere, anywhere),
        scratch_shapes=[
            pltpu.VMEM((2 * hid, width), BF16),
            pltpu.VMEM((2, 3 * hid, 4 * qr), BF16),
            pltpu.VMEM((n, 2, SRC, ROWS, w), BF16),
            pltpu.VMEM((n, 2, SRC, ROWS, w), BF16),
            pltpu.VMEM((n, 2, SRC, ROWS, w), BF16),
            pltpu.VMEM((n, 2, SRC, ROWS, w), BF16),
            pltpu.VMEM((n, 2, 2, ROWS, w), BF16),
            pltpu.VMEM((n, 2, SRC, ROWS, w), BF16),
            pltpu.VMEM((n, 2, NZ, PAD, w), BF16),
            pltpu.VMEM((n, 7, 2, PAD, w), BF16),
            pltpu.VMEM((n, 7, 2, PAD, w), BF16),
            pltpu.VMEM((n, PAD, w), BF16),
            pltpu.VMEM((n, PAD, w), BF16),
            pltpu.VMEM((2, 4, SRC, ROWS, w), BF16),
            pltpu.VMEM((2, 4, SRC, ROWS, w), BF16),
            pltpu.VMEM((n, 2 * hid, w), BF16),
            pltpu.VMEM((n, hid, w), BF16),
            dma((2,)), dma((2, 2)), dma((n,)), dma((n,)), dma((n,)), dma((n,)), dma((n,)), dma((n,)),
            dma((n, 7)), dma((n, 7)), dma((n,)), dma((n,)), dma((n, 3)),
        ],
        compiler_params=pltpu.CompilerParams(collective_id=1, has_side_effects=True, vmem_limit_bytes=VMEM_LIMIT),
    )(act, act_t, st, w_gate[0], w_up[0], rows)
    return (d_tok, d_gate[None], d_up[None], d_down[None])


def solution(mesh):
    rows = P(("dp", "expert"), None)
    weights = P("expert", "dp", None)
    return jax.shard_map(
        per_device,
        mesh=mesh,
        in_specs=(rows, rows, rows, rows, weights, weights, weights),
        out_specs=(rows, weights, weights, weights),
        check_vma=False,
    )
```

time: 484 us -> 292 us (0.60); the launches traced: 475 us -> 291 us
  Pallas kernels: 0 us -> 278 us
  waiting for transfers between devices: 200 us -> 0 us
  blocking collectives: 121 us -> 0 us
  matrix products: 64.6 us -> 0 us
  local copies, waits for them, and re-layouts: 62.1 us -> 9.76 us
  between operations: 14.4 us -> 0.69 us
  starting transfers between devices: 11.7 us -> 0 us
    pallas_call x0 -> x2, Pallas kernels: none -> 278 us  [the longest x1 166 us: per_device(): pl.pallas_call(route_stage, out_shape=(shape((n, 4, SRC, ROWS, w), BF16),...]
    all_to_all x2 -> x0, blocking collectives: 121 us -> none  [the longest x1 64 us: per_device(): lax.all_to_all(input_send, 'expert', split_axis=0, concat_axis=0, tiled=T...]
    all_gather x2 -> x0, waiting for transfers between devices: 84.4 us -> none  [the longest x1 65.9 us: per_device(): lax.all_gather(grad_recv, 'dp', axis=1, tiled=True)]
    reduce_scatter x1 -> x0, waiting for transfers between devices: 84.3 us -> none  [per_device(): lax.psum_scatter(held.astype(jnp.bfloat16), 'dp', scatter_dimension=1, ti...]
    dot_general x11 -> x0, matrix products: 64.6 us -> none  [the longest x1 11.4 us: per_device(): jnp.einsum('rf,fd->rd', d_up_act, up_w, preferred_element_type=jnp.float32)]
    all_to_all x1 -> x0, waiting for transfers between devices: 31.7 us -> none  [per_device(): lax.all_to_all(slot_total[:, 0].astype(jnp.bfloat16), 'expert', split_axi...]
    all_gather x2 -> x0, local copies, waits for them, and re-layouts: 22.8 us -> none  [the longest x1 11.6 us: per_device(): lax.all_gather(grad_recv, 'dp', axis=1, tiled=True)]
    reshape x2 -> x0, local copies, waits for them, and re-layouts: 13.4 us -> none  [the longest x1 13.3 us: per_device(): partial_sum.astype(jnp.bfloat16)]
  transfers between devices with their start and end apart: 4 -> 0, of which waited for: 4 -> 0; matrix products, arithmetic and copies ran while one was open for 10% -> 0% of each run, Pallas kernels for 0% -> 0%
where the time goes in v1:
time: 292 us; the launch traced here: 291 us
  Pallas kernels  278 us (95%)
  local copies, waits for them, and re-layouts  9.76 us (3%)
    pallas_call x1, Pallas kernels, per_device(): pl.pallas_call(route_stage, out_shape=(shape((n, 4, SRC, ROWS, w), BF16),...  166 us
    pallas_call x1, Pallas kernels, per_device(): pl.pallas_call(return_stage, out_shape=(shape((TOK, width), BF16),) + (sh...  112 us
    unnamed x8, local copies, waits for them, and re-layouts  7.56 us

profile of v1, /device:TPU:1, one launch (start us, length us, event | category | flops | bytes accessed | tf_op | source)
XLA Modules:
  0.0 290.9 jit_solution(538040287669475267)
XLA Ops:
  0.7 0.1 iota.11
  0.7 0.1 iota.12
  0.8 0.7 fusion.3
  1.5 0.7 fusion.2
  2.2 0.1 broadcast_in_dim.25
  2.3 0.6 broadcast_select_fusion.info
  2.9 0.9 pad.11
  3.9 0.9 pad.12
  4.9 0.8 pad_maximum_fusion.tok
  5.7 166.0 %shard_map.102 = (bf16[16,4,8,32,512]{4,3,2,1,0:T(8,128)(2,1)}, bf16[576,1024]{1,0:T(8,128)(2,1)}, bf16[1024,384]{1,0:T(8,128)(2,1)}, bf16[3,256,256]{2,1,0:T(8,128)(2,1)}) custom-call(bf16[16,32,512]{2,1,0:T(8,128)(2,1)} %pad_maximum_fusion.tok, bf16[16,128]{1,0:T(8,128)(2,1)} %broadcast_select_fusion.info, bf16[192,4096]{1,0:T(8,128)(2,1)} %bitcast.19, ...), custom_call_target="tpu_custom_call" | custom-call | tf_op jit(solution)/shard_map/pallas_call | solution.py:482
  171.7 111.6 %shard_map.103 = (bf16[24,4096]{1,0:T(8,128)(2,1)}, bf16[192,4096]{1,0:T(8,128)(2,1)}, bf16[192,4096]{1,0:T(8,128)(2,1)}, bf16[192,4096]{1,0:T(8,128)(2,1)}) custom-call(bf16[1024,384]{1,0:T(8,128)(2,1)} %get-tuple-element.12.act, bf16[576,1024]{1,0:T(8,128)(2,1)} %get-tuple-element.13.act_t, bf16[3,256,256]{2,1,0:T(8,128)(2,1)} %get-tuple-element.14.st, ...), custom_call_target="tpu_custom_call" | custom-call | tf_op jit(solution)/shard_map/pallas_call | solution.py:505
  283.3 1.6 copy.21
  284.9 0.0 copy-start.1
  284.9 2.8 copy.22
  287.8 0.0 copy-done.1
  287.8 0.0 copy-start
  287.8 1.1 copy.23
  288.9 0.8 copy-done
  289.7 1.1 copy.24
  (3 shorter events, 0.1 us)
Async XLA Ops:
  284.9 2.8 copy-start.1
  287.8 2.0 copy-start

commit v2 on v1

--- a/solution.py
+++ b/solution.py
@@ -15,6 +15,9 @@
 PAD = 32
 SRC = NX * NCORE
 ROWS = NZ * CAP
+LAG, LATE_LAG = 2, 3
+RLAG, RLATE_LAG = 2, 2
+WIDTH = 256
 
 
 class Place:
@@ -150,17 +153,17 @@
 
         for k in (1, 2):
 
-            @pl.when(t == k)
+            @pl.when(t == k * LAG)
             def _(k=k):
                 z_wait(rb, k, r_r)
                 z_hop(rb, k + 1, one, r_r)
 
-        @pl.when(t == 3)
+        @pl.when(t == 3 * LAG)
         def _():
             z_wait(rb, 3, r_r)
             z_last(rb, 0, one, r_r)
 
-        @pl.when(t == 4)
+        @pl.when(t == 4 * LAG)
         def _():
             await_(rb.at[:, 0], r_r.at[6])
             select_matrices()
@@ -197,7 +200,7 @@
             st_out[role] = sm[0, role].astype(F32).T.astype(BF16)
 
     def step(t, carry):
-        i6, i5, i4, i3, i2, i1 = (t - k for k in (6, 5, 4, 3, 2, 1))
+        i6, i5, i4, i3, i2, i1 = (t - k * LAG for k in (6, 5, 4, 3, 2, 1))
 
         @when(i6, n)
         def _():
@@ -244,7 +247,7 @@
             await_(tok.at[t], a_r.at[t])
             z_hop(zbuf.at[t], 1, lambda j: z_s.at[t], z_r.at[t])
 
-        i8 = t - 8
+        i8 = t - 6 * LAG - LATE_LAG
 
         @pl.when(i8 == 0)
         def _():
@@ -279,7 +282,7 @@
 
         return carry
 
-    lax.fori_loop(0, n + 8, step, 0)
+    lax.fori_loop(0, n + 6 * LAG + LATE_LAG, step, 0)
 
     for q in range(4):
         at = pl.ds(q * SRC * ROWS, SRC * ROWS)
@@ -342,7 +345,8 @@
         send(src, zr.at[i, j], z_s.at[i, j], z_r.at[i, j], p.at(z=p.zz(d)))
 
     def step(t, carry):
-        i1, i2, i3, i4, i5, i6, i7, i8 = (t - k for k in range(1, 9))
+        i1, i2, i3, i4, i5, i6, i7, i8 = (t - RLATE_LAG - k * RLAG for k in range(8))
+        m = t - RLATE_LAG
 
         @when(t, n)
         def _():
@@ -421,29 +425,29 @@
             value = zs[i8, 6, 0].astype(F32) + tail_in[i8].astype(F32)
             d_tok[:, pl.ds(pl.multiple_of(i8 * w, w), w)] = value[0:TOK].astype(BF16)
 
-        @when(t, n)
-        def _():
-            slot = lax.rem(t, 2)
-
-            @pl.when(t + 1 < n)
+        @when(m, n)
+        def _():
+            slot = lax.rem(m, 2)
+
+            @pl.when(m + 1 < n)
             def _():
-                fetch(t + 1, 1 - slot)
+                fetch(m + 1, 1 - slot)
 
             await_(xr.at[slot], in_s.at[slot, 0])
             await_(gr.at[slot], in_s.at[slot, 1])
             a = acts[slot]
             x_all = xr[slot].reshape(4 * qr, w)
             g_all = gr[slot].reshape(4 * qr, w)
-            dw_gu[t] = dot(a[0 : 2 * hid], x_all).astype(BF16)
-            dw_d[t] = dot(a[2 * hid : 3 * hid], g_all).astype(BF16)
-            at = pl.ds(pl.multiple_of(t * w, w), w)
-            pltpu.make_async_copy(dw_gu.at[t, pl.ds(0, hid)], d_gate.at[:, at], o_s.at[t, 0]).start()
-            pltpu.make_async_copy(dw_gu.at[t, pl.ds(hid, hid)], d_up.at[:, at], o_s.at[t, 1]).start()
-            pltpu.make_async_copy(dw_d.at[t], d_down.at[:, at], o_s.at[t, 2]).start()
+            dw_gu[m] = dot(a[0 : 2 * hid], x_all).astype(BF16)
+            dw_d[m] = dot(a[2 * hid : 3 * hid], g_all).astype(BF16)
+            at = pl.ds(pl.multiple_of(m * w, w), w)
+            pltpu.make_async_copy(dw_gu.at[m, pl.ds(0, hid)], d_gate.at[:, at], o_s.at[m, 0]).start()
+            pltpu.make_async_copy(dw_gu.at[m, pl.ds(hid, hid)], d_up.at[:, at], o_s.at[m, 1]).start()
+            pltpu.make_async_copy(dw_d.at[m], d_down.at[:, at], o_s.at[m, 2]).start()
 
         return carry
 
-    lax.fori_loop(0, n + 8, step, 0)
+    lax.fori_loop(0, n + RLATE_LAG + 7 * RLAG, step, 0)
 
     @pl.loop(0, n)
     def _(i):
@@ -459,7 +463,7 @@
 
 def per_device(tokens, out_grad, routes, gates, w_gate, w_up, w_down):
     width = tokens.shape[1]
-    w = 512
+    w = WIDTH
     nc = width // w
     n = 2 * nc
     hid = w_gate.shape[1]

time: 292 us -> 241 us (0.83)
  Pallas kernels: 278 us -> 227 us
    pallas_call x1, Pallas kernels: 166 us -> 140 us  [per_device(): pl.pallas_call(route_stage, out_shape=(shape((n, 4, SRC, ROWS, w), BF16),...]
    pallas_call x1, Pallas kernels: 112 us -> 87.5 us  [per_device(): pl.pallas_call(return_stage, out_shape=(shape((TOK, width), BF16),) + (sh...]
where the time goes in v2:
time: 241 us; the launch traced here: 240 us
  Pallas kernels  227 us (94%)
  local copies, waits for them, and re-layouts  9.77 us (4%)
  other arithmetic  2.83 us (1%)
    pallas_call x1, Pallas kernels, per_device(): pl.pallas_call(route_stage, out_shape=(shape((n, 4, SRC, ROWS, w), BF16),...  140 us
    pallas_call x1, Pallas kernels, per_device(): pl.pallas_call(return_stage, out_shape=(shape((TOK, width), BF16),) + (sh...  87.5 us
    unnamed x8, local copies, waits for them, and re-layouts  7.56 us

profile of v2, /device:TPU:1, one launch (start us, length us, event | category | flops | bytes accessed | tf_op | source)
XLA Modules:
  0.0 240.5 jit_solution(5239239386647895787)
XLA Ops:
  0.7 0.1 iota.11
  0.7 0.1 iota.12
  0.8 0.7 fusion.3
  1.5 0.7 fusion.2
  2.2 0.1 broadcast_in_dim.25
  2.3 0.6 broadcast_select_fusion.info
  2.9 0.9 pad.11
  3.9 0.9 pad.12
  4.8 0.1 bitcast_bitcast_fusion
  4.9 0.8 pad_maximum_fusion.tok
  5.7 139.7 %shard_map.102 = (bf16[32,4,8,32,256]{4,3,2,1,0:T(8,128)(2,1)}, bf16[576,1024]{1,0:T(8,128)(2,1)}, bf16[1024,384]{1,0:T(8,128)(2,1)}, bf16[3,256,256]{2,1,0:T(8,128)(2,1)}) custom-call(bf16[32,32,256]{2,1,0:T(8,128)(2,1)} %pad_maximum_fusion.tok, bf16[16,128]{1,0:T(8,128)(2,1)} %broadcast_select_fusion.info, bf16[192,4096]{1,0:T(8,128)(2,1)} %bitcast.19, ...), custom_call_target="tpu_custom_call" | custom-call | tf_op jit(solution)/shard_map/pallas_call | solution.py:486
  145.4 87.5 %shard_map.103 = (bf16[24,4096]{1,0:T(8,128)(2,1)}, bf16[192,4096]{1,0:T(8,128)(2,1)}, bf16[192,4096]{1,0:T(8,128)(2,1)}, bf16[192,4096]{1,0:T(8,128)(2,1)}) custom-call(bf16[1024,384]{1,0:T(8,128)(2,1)} %get-tuple-element.12.act, bf16[576,1024]{1,0:T(8,128)(2,1)} %get-tuple-element.13.act_t, bf16[3,256,256]{2,1,0:T(8,128)(2,1)} %get-tuple-element.14.st, ...), custom_call_target="tpu_custom_call" | custom-call | tf_op jit(solution)/shard_map/pallas_call | solution.py:509
  232.9 1.6 copy.21
  234.5 0.0 copy-start.1
  234.5 2.8 %copy.22 = bf16[1,192,4096]{2,1,0:T(8,128)(2,1)} copy(bf16[1,192,4096]{2,1,0:T(8,128)(2,1)} %bitcast.25) | data formatting | bytes 3145728
  237.4 0.0 copy-done.1
  237.4 0.0 copy-start
  237.4 1.1 copy.23
  238.5 0.8 copy-done
  239.3 1.1 copy.24
  (2 shorter events, 0.0 us)
Async XLA Ops:
  234.5 2.8 %copy-start.1 = (bf16[192,4096]{1,0:T(8,128)(2,1)S(1)}, bf16[192,4096]{1,0:T(8,128)(2,1)}, u32[]{:S(2)}) copy-start(bf16[192,4096]{1,0:T(8,128)(2,1)} %get-tuple-element.18) | copy-start | bytes 4718596
  237.4 2.0 copy-start

commit v3 on v0

v3 whole, which is shorter than its diff:
```python
import jax
import jax.numpy as jnp
from jax import lax
from jax.experimental import pallas as pl
from jax.experimental.pallas import tpu as pltpu
from jax.sharding import PartitionSpec as P

MESH = pl.DeviceIdType.MESH
F32, BF16 = jnp.float32, jnp.bfloat16
VMEM_LIMIT = 67043328

NY, NX, NZ, NCORE = 4, 4, 8, 2
CAP = 4
TOK = 24
PAD = 32
SRC = NX * NCORE
ROWS = NZ * CAP
QUARTER = SRC * ROWS
WIDTH = 256
LAG, LATE_LAG = 2, 5
RLATE_LAG, RLAG = 4, 2
DW_LAG = 2
REAL = pl.ds(0, TOK)


class Place:
    def __init__(self):
        self.y = lax.axis_index("dp")
        e = lax.axis_index("expert")
        self.c = lax.rem(e, NCORE)
        self.z = lax.rem(lax.div(e, NCORE), NZ)
        self.x = lax.div(e, NCORE * NZ)

    @staticmethod
    def first(i):
        return i + 1 - 2 * lax.rem(i, 2)

    @staticmethod
    def second(i):
        return 3 - i

    def pick(self, i, s):
        return (1 - s) * self.first(i) + s * self.second(i)

    def at(self, y=None, x=None, z=None, c=None):
        y = self.y if y is None else y
        x = self.x if x is None else x
        z = self.z if z is None else z
        c = self.c if c is None else c
        return (y, (x * NZ + z) * NCORE + c)

    def zz(self, d):
        return lax.rem(self.z + d + NZ, NZ)

    def enter(self):
        sem = pltpu.get_barrier_semaphore()
        peers = [self.at(y=self.first(self.y)), self.at(y=self.second(self.y)), self.at(c=1 - self.c)]
        peers += [self.at(z=self.zz(d)) for d in (1, -1, 2, -2)]
        for x in (self.first(self.x), self.second(self.x)):
            peers += [self.at(x=x, c=0), self.at(x=x, c=1)]
        for p in peers:
            pl.semaphore_signal(sem, inc=1, device_id=p, device_id_type=MESH)
        pl.semaphore_wait(sem, len(peers))


def send(src, dst, ssem, rsem, device):
    pltpu.make_async_remote_copy(
        src_ref=src, dst_ref=dst, send_sem=ssem, recv_sem=rsem, device_id=device, device_id_type=MESH
    ).start()


def await_(ref, sem):
    pltpu.make_async_copy(ref, ref, sem).wait()


def when(i, n):
    return pl.when(jnp.logical_and(i >= 0, i < n))


def dot(a, b, dims=((1,), (0,))):
    return lax.dot_general(a, b, (dims, ((), ())), preferred_element_type=F32)


def slot_exchange(p, s, sel, fwd, into, send_sem, fwd_recv, recv_sem):
    mine = p.c
    send(sel.at[:, pl.ds(6, 2)], fwd, send_sem, fwd_recv, p.at(x=p.pick(p.x, s)))
    for d, x in ((1, p.first(p.x)), (2, p.second(p.x))):
        for c in range(NCORE):
            send(sel.at[:, d * 2 + c], into.at[:, d * 2 + mine], send_sem, recv_sem, p.at(x=x, c=c))
    send(sel.at[:, 1 - mine], into.at[:, mine], send_sem, recv_sem, p.at(c=1 - mine))


def pass_on(p, s, fwd, into, fwd_send, recv_sem):
    for c in range(NCORE):
        send(fwd.at[:, c], into.at[:, 6 + p.c], fwd_send, recv_sem, p.at(x=p.pick(p.x, 1 - s), c=c))


def gather_near(p, block, ssem, rsem):
    mine = block(p.z)
    for j, d in enumerate((2, -2, 1, -1)):
        send(mine, mine, ssem(j), rsem.at[j], p.at(z=p.zz(d)))


def gather_far(p, s, block, ssem, rsem):
    for j in (0, 1):
        await_(block(p.z), rsem.at[j])
    d = 2 - 4 * s
    far = block(p.zz(-d))
    send(far, far, ssem(6), rsem.at[6], p.at(z=p.zz(d)))
    for j, d in enumerate((1, -1)):
        passed = block(p.zz(-2 * d))
        send(passed, passed, ssem(4 + j), rsem.at[4 + j], p.at(z=p.zz(d)))


def gather_wait(p, block, rsem):
    for j in range(2, 7):
        await_(block(p.z), rsem.at[j])


def quarter(pos, s):
    return (0, 1 + s, 2 - s, 3)[pos]


def select_matrices(p, rb, sm, st):
    lane = lax.broadcasted_iota(jnp.int32, (128, 128), 1)
    sub = lax.broadcasted_iota(jnp.int32, (128, 128), 0)
    before = jnp.where(jnp.logical_and(sub < lane, lax.div(sub, PAD) == lax.div(lane, PAD)), 1.0, 0.0).astype(BF16)
    r_row = lax.broadcasted_iota(jnp.int32, (ROWS, 128), 0)
    r_lane = lax.broadcasted_iota(jnp.int32, (ROWS, 128), 1)
    row_z, row_slot = lax.div(r_row, CAP), lax.rem(r_row, CAP).astype(F32)
    xs = (p.x, p.first(p.x), p.second(p.x), lax.rem(p.x + 2, NX))
    spread = lambda v: jnp.broadcast_to(v, (ROWS, 128))
    for role in range(3):
        for zh in range(2):
            both = rb[role, 4 * zh].astype(F32)
            for q in range(1, 4):
                both = both + rb[role, 4 * zh + q].astype(F32)
            route, gate = both[0:8].astype(jnp.int32), both[8:16]
            chosen, value = [], []
            for d in range(4):
                for c in range(NCORE):
                    hit = route == (xs[d] * NZ + p.z) * NCORE + c + 1
                    chosen.append(jnp.sum(jnp.where(hit, 1.0, 0.0), axis=0, keepdims=True))
                    value.append(jnp.sum(jnp.where(hit, gate, 0.0), axis=0, keepdims=True))
            chosen = jnp.concatenate(chosen, axis=0)
            earlier = dot(chosen.astype(BF16), before)
            same_z = row_z == 4 * zh + lax.div(r_lane, PAD)
            for e in range(SRC):
                hit = jnp.logical_and(spread(chosen[e : e + 1]) > 0.5, spread(earlier[e : e + 1]) == row_slot)
                hit = jnp.logical_and(same_z, hit)
                rows, cols = pl.ds(e * ROWS, ROWS), pl.ds(zh * 128, 128)
                sm[0, role, rows, cols] = jnp.where(hit, 1.0, 0.0).astype(BF16)
                sm[1, role, rows, cols] = jnp.where(hit, spread(value[e]), 0.0).astype(BF16)
        st[role] = sm[0, role].astype(F32).T.astype(BF16)


def layer(tok, ograd, info, wg, wu, wd, d_tok, d_gate, d_up, d_down,
          zbuf, sel, fwd, rows, wgu, wdn, acc_gu, acc_d, sm, st, rb, act_t, act,
          got, back, fwd2, zr, tail, tail_in, dw_gu, dw_d,
          sem_l, a_s, a_r, z_s, z_r, x_s, x_r, f_s, f_r, l_s, l_r, r_s, r_r,
          l2_s, l2_r, x2_s, x2_r, f2_s, f2_r, z2_s, z2_r, e_s, e_r, o_s):
    p = Place()
    n, w = zbuf.shape[0], zbuf.shape[-1]
    half = n // 2
    hid = wg.shape[0]
    qr = QUARTER

    def cols(i):
        return pl.ds(pl.multiple_of(i * w, w), w)

    own_info = pltpu.make_async_copy(info, rb.at[0, p.z], sem_l.at[0])
    own_info.start()
    for k, ref in enumerate((tok, ograd)):

        @pl.loop(0, half)
        def _(j, k=k, ref=ref):
            pltpu.make_async_copy(ref.at[:, cols(j)], zbuf.at[k * half + j, 0, p.z, REAL], sem_l.at[1 + k]).start()

    p.enter()
    send(info, rb.at[1, p.z], r_s.at[7], r_r.at[7], p.at(y=p.first(p.y)))
    send(info, rb.at[2, p.z], r_s.at[8], r_r.at[8], p.at(y=p.second(p.y)))
    for k, ref in enumerate((tok, ograd)):

        @pl.loop(0, half)
        def _(j, k=k, ref=ref):
            i = k * half + j
            to = p.at(y=p.pick(p.y, lax.rem(j, 2)))
            send(ref.at[:, cols(j)], zbuf.at[i, 1, p.z, REAL], a_s.at[i], a_r.at[i], to)

    loads = [
        pltpu.make_async_copy(wg, wgu.at[pl.ds(0, hid)], sem_l.at[3]),
        pltpu.make_async_copy(wu, wgu.at[pl.ds(hid, hid)], sem_l.at[4]),
        pltpu.make_async_copy(wd, wdn, sem_l.at[5]),
    ]
    for cp in loads:
        cp.start()

    zbuf[:, :, :, pl.ds(TOK, PAD - TOK), :] = jnp.zeros((n, 2, NZ, PAD - TOK, w), BF16)
    acc_gu[...] = jnp.zeros_like(acc_gu)
    acc_d[...] = jnp.zeros_like(acc_d)

    info_block = lambda z: rb.at[:, z]
    token_block = lambda i: lambda z: zbuf.at[i, :, z, REAL]

    def step(t, carry):
        i_far, i_sel, i_pass, i_late = (t - k * LAG for k in range(1, 5))
        i_mul = t - 4 * LAG - LATE_LAG

        @pl.when(t == 0)
        def _():
            own_info.wait()
            await_(info, r_r.at[7])
            await_(info, r_r.at[8])
            gather_near(p, info_block, lambda j: r_s.at[j], r_r)
            await_(tok, sem_l.at[1])

        @pl.when(t == LAG)
        def _():
            gather_far(p, 0, info_block, lambda j: r_s.at[j], r_r)

        @pl.when(t == 2 * LAG)
        def _():
            gather_wait(p, info_block, r_r)
            select_matrices(p, rb, sm, st)

        @when(t, n)
        def _():
            @pl.when(t == half)
            def _():
                await_(ograd, sem_l.at[2])

            await_(tok.at[:, pl.ds(0, w)], a_r.at[t])
            gather_near(p, token_block(t), lambda j: z_s.at[t], z_r.at[t])

        @when(i_far, n)
        def _():
            gather_far(p, lax.rem(i_far, 2), token_block(i_far), lambda j: z_s.at[i_far], z_r.at[i_far])

        @when(i_sel, n)
        def _():
            s = lax.rem(i_sel, 2)
            which = lax.div(i_sel, half)
            gather_wait(p, token_block(i_sel), z_r.at[i_sel])
            for ys, role in ((0, 0), (1, 1 + s)):
                chosen = dot(sm[which, role], zbuf[i_sel, ys].reshape(NZ * PAD, w)).astype(BF16)
                sel[i_sel, ys] = chosen.reshape(SRC, ROWS, w)
            slot_exchange(p, s, sel.at[i_sel], fwd.at[i_sel], rows.at[i_sel, 0], x_s.at[i_sel], f_r.at[i_sel], x_r.at[i_sel])
            rows[i_sel, 0, :, p.c] = sel[i_sel, :, p.c]

        @when(i_pass, n)
        def _():
            await_(fwd.at[i_pass], f_r.at[i_pass])
            pass_on(p, lax.rem(i_pass, 2), fwd.at[i_pass], rows.at[i_pass, 0], f_s.at[i_pass], x_r.at[i_pass])

        @when(i_late, n)
        def _():
            await_(rows.at[i_late, 0, :, pl.ds(0, 7)], x_r.at[i_late])
            late = p.at(y=p.pick(p.y, 1 - lax.rem(i_late, 2)))
            send(rows.at[i_late, 0], rows.at[i_late, 1], l_s.at[i_late], l_r.at[i_late], late)

        @pl.when(i_mul == 0)
        def _():
            for cp in loads:
                cp.wait()

        @when(i_mul, n)
        def _():
            s = lax.rem(i_mul, 2)
            await_(rows.at[i_mul, 1], l_r.at[i_mul])

            def multiply(acc, weights):
                part = weights[:, cols(lax.rem(i_mul, half))]
                for h in range(2):
                    for ys in range(2):
                        at = pl.ds(pl.multiple_of(quarter(2 * h + ys, s) * qr, qr), qr)
                        acc[:, at] += dot(part, rows[i_mul, h, ys].reshape(qr, w), ((1,), (1,)))

            @pl.when(i_mul < half)
            def _():
                multiply(acc_gu, wgu)

            @pl.when(i_mul >= half)
            def _():
                multiply(acc_d, wdn)

        return carry

    lax.fori_loop(0, n + 4 * LAG + LATE_LAG, step, 0)

    for q in range(4):
        at = pl.ds(q * qr, qr)
        swapped = pl.ds((0, 2, 1, 3)[q] * qr, qr)
        gate_pre, up_pre, d_hidden = acc_gu[0:hid, at], acc_gu[hid : 2 * hid, at], acc_d[:, at]
        sig = jax.nn.sigmoid(gate_pre)
        silu = gate_pre * sig
        d_up_act = d_hidden * silu
        d_gate_act = d_hidden * up_pre * sig * (1.0 + gate_pre * (1.0 - sig))
        both = jnp.concatenate([d_gate_act, d_up_act], axis=0)
        act[at, :] = both.T.astype(BF16)
        both, hidden = both.astype(BF16), (silu * up_pre).astype(BF16)
        for order, to in ((0, at), (1, swapped)):
            act_t[order, 0 : 2 * hid, to] = both
            act_t[order, 2 * hid : 3 * hid, to] = hidden

    @pl.loop(0, n)
    def _(i):
        await_(zbuf.at[i, :, pl.ds(0, 7), REAL], z_s.at[i])
        await_(sel.at[i, :, pl.ds(0, 7)], x_s.at[i])

    def part(i):
        return zbuf.at[i]

    def keep(i):
        return zbuf.at[half + i]

    def own(i):
        return sel.at[i]

    def sums(i):
        return sel.at[half + i]

    def back_step(t, carry):
        i_sum, i_pass, i_tok, i_far, i_end, i_out = (t - RLATE_LAG - k * RLAG for k in range(6))
        i_dw = t - DW_LAG

        @when(t, half)
        def _():
            s = lax.rem(t, 2)
            weights = wgu[:, cols(t)]
            for pos in (2, 3, 0, 1):
                a = act[pl.ds(pl.multiple_of(quarter(pos, s) * qr, qr), qr), :]
                value = dot(a, weights).astype(BF16).reshape(SRC, ROWS, w)
                if pos >= 2:
                    part(t)[pos - 2] = value
                else:
                    keep(t)[pos] = value
                if pos == 3:
                    send(part(t), got.at[t], l2_s.at[t], l2_r.at[t], p.at(y=p.pick(p.y, 1 - s)))

        @when(i_sum, half)
        def _():
            s = lax.rem(i_sum, 2)
            await_(got.at[i_sum], l2_r.at[i_sum])
            total = keep(i_sum)
            total[...] = (total[...].astype(F32) + got[i_sum].astype(F32)).astype(BF16)
            slot_exchange(p, s, total, fwd2.at[i_sum], back.at[i_sum], x2_s.at[i_sum], f2_r.at[i_sum], x2_r.at[i_sum])
            back[i_sum, :, p.c] = total[:, p.c]

        @when(i_pass, half)
        def _():
            await_(fwd2.at[i_pass], f2_r.at[i_pass])
            pass_on(p, lax.rem(i_pass, 2), fwd2.at[i_pass], back.at[i_pass], f2_s.at[i_pass], x2_r.at[i_pass])

        def z_send(i, j, src, d):
            send(src, zr.at[i, j], z2_s.at[i], z2_r.at[i, j], p.at(z=p.zz(d)))

        @when(i_tok, half)
        def _():
            s = lax.rem(i_tok, 2)
            await_(back.at[i_tok, :, pl.ds(0, 7)], x2_r.at[i_tok])
            mine = own(i_tok)
            for ys, role in ((0, 0), (1, 1 + s)):
                value = dot(st[role], back[i_tok, ys].reshape(qr, w)).astype(BF16)
                mine[ys] = value.reshape(NZ, PAD, w)
            d = 4 * s - 2
            z_send(i_tok, 2, mine.at[:, p.zz(4), REAL], d)
            for j, d in enumerate((-1, 1)):
                z_send(i_tok, j, mine.at[:, p.zz(3 * d), REAL], d)
                z_send(i_tok, 3 + j, mine.at[:, p.zz(d), REAL], d)

        @when(i_far, half)
        def _():
            s = lax.rem(i_far, 2)
            for j in range(3):
                await_(zr.at[i_far, j], z2_r.at[i_far, j])
            four = zr[i_far, 2].astype(F32)
            for j, d in enumerate((-2, 2)):
                value = own(i_far)[:, p.zz(d), REAL].astype(F32) + zr[i_far, j].astype(F32)
                value = value + jnp.where(s == j, four, 0.0)
                sums(i_far)[:, j, REAL] = value.astype(BF16)
                z_send(i_far, 5 + j, sums(i_far).at[:, j, REAL], d)

        @when(i_end, half)
        def _():
            for j in range(3, 7):
                await_(zr.at[i_end, j], z2_r.at[i_end, j])
            value = own(i_end)[:, p.z, REAL].astype(F32)
            for j in range(3, 7):
                value = value + zr[i_end, j].astype(F32)
            tail[i_end] = value.astype(BF16)
            send(tail.at[i_end, 1], tail_in.at[i_end], e_s.at[i_end], e_r.at[i_end], p.at(y=p.pick(p.y, lax.rem(i_end, 2))))

        @when(i_out, half)
        def _():
            await_(tail_in.at[i_out], e_r.at[i_out])
            value = tail[i_out, 0].astype(F32) + tail_in[i_out].astype(F32)
            d_tok[:, cols(i_out)] = value.astype(BF16)

        @when(i_dw, half)
        def _():
            slot = lax.rem(i_dw, 2)
            at = cols(i_dw)
            copies = (
                pltpu.make_async_copy(dw_gu.at[slot, pl.ds(0, hid)], d_gate.at[:, at], o_s.at[slot, 0]),
                pltpu.make_async_copy(dw_gu.at[slot, pl.ds(hid, hid)], d_up.at[:, at], o_s.at[slot, 1]),
                pltpu.make_async_copy(dw_d.at[slot], d_down.at[:, at], o_s.at[slot, 2]),
            )

            @pl.when(i_dw >= 2)
            def _():
                for cp in copies:
                    cp.wait()

            a = act_t.at[slot]
            dw_gu[slot] = dot(a[0 : 2 * hid], rows[i_dw].reshape(4 * qr, w)).astype(BF16)
            dw_d[slot] = dot(a[2 * hid : 3 * hid], rows[half + i_dw].reshape(4 * qr, w)).astype(BF16)
            for cp in copies:
                cp.start()

        return carry

    lax.fori_loop(0, half + RLATE_LAG + 5 * RLAG, back_step, 0)

    @pl.loop(0, n)
    def _(i):
        await_(tok.at[:, pl.ds(0, w)], a_s.at[i])
        await_(fwd.at[i], f_s.at[i])
        await_(rows.at[i, 0], l_s.at[i])

    @pl.loop(0, half)
    def _(i):
        await_(part(i), l2_s.at[i])
        await_(back.at[i, :, pl.ds(0, 7)], x2_s.at[i])
        await_(fwd2.at[i], f2_s.at[i])
        await_(zr.at[i], z2_s.at[i])
        await_(tail_in.at[i], e_s.at[i])

    for slot in range(2):
        for j in range(3):
            await_(dw_d.at[slot], o_s.at[slot, j])
    for j in range(7):
        await_(rb.at[:, 0], r_s.at[j])
    await_(info, r_s.at[7])
    await_(info, r_s.at[8])


def per_device(tokens, out_grad, routes, gates, w_gate, w_up, w_down):
    width = tokens.shape[1]
    w = WIDTH
    half = width // w
    n = 2 * half
    hid = w_gate.shape[1]
    qr = QUARTER
    z = lax.rem(lax.div(lax.axis_index("expert"), NCORE), NZ)

    info = jnp.concatenate([(routes + 1).astype(BF16).T, gates.T], axis=0)
    info = jnp.pad(info, ((0, 0), (0, PAD - TOK)))
    info = jnp.where(lax.broadcasted_iota(jnp.int32, (16, 4, PAD), 1) == lax.rem(z, 4), info[:, None, :], 0).reshape(16, 128)

    anywhere = pl.BlockSpec(memory_space=pl.ANY)
    vmem = pl.BlockSpec(memory_space=pltpu.VMEM)
    dma = pltpu.SemaphoreType.DMA
    shape = jax.ShapeDtypeStruct
    d_tok, d_gate, d_up, d_down = pl.pallas_call(
        layer,
        out_shape=(shape((TOK, width), BF16),) + (shape((hid, width), BF16),) * 3,
        in_specs=[anywhere, anywhere, vmem, anywhere, anywhere, anywhere],
        out_specs=(vmem, anywhere, anywhere, anywhere),
        scratch_shapes=[
            pltpu.VMEM((n, 2, NZ, PAD, w), BF16),
            pltpu.VMEM((n, 2, SRC, ROWS, w), BF16),
            pltpu.VMEM((n, 2, 2, ROWS, w), BF16),
            pltpu.VMEM((n, 2, 2, SRC, ROWS, w), BF16),
            pltpu.VMEM((2 * hid, width), BF16),
            pltpu.VMEM((hid, width), BF16),
            pltpu.VMEM((2 * hid, 4 * qr), F32),
            pltpu.VMEM((hid, 4 * qr), F32),
            pltpu.VMEM((2, 3, qr, qr), BF16),
            pltpu.VMEM((3, qr, qr), BF16),
            pltpu.VMEM((3, NZ, 16, 128), BF16),
            pltpu.VMEM((2, 3 * hid, 4 * qr), BF16),
            pltpu.VMEM((4 * qr, 2 * hid), BF16),
            pltpu.VMEM((half, 2, SRC, ROWS, w), BF16),
            pltpu.VMEM((half, 2, SRC, ROWS, w), BF16),
            pltpu.VMEM((half, 2, 2, ROWS, w), BF16),
            pltpu.VMEM((half, 7, 2, TOK, w), BF16),
            pltpu.VMEM((half, 2, TOK, w), BF16),
            pltpu.VMEM((half, TOK, w), BF16),
            pltpu.VMEM((2, 2 * hid, w), BF16),
            pltpu.VMEM((2, hid, w), BF16),
            dma((6,)), dma((n,)), dma((n,)), dma((n,)), dma((n, 7)), dma((n,)), dma((n,)), dma((n,)), dma((n,)),
            dma((n,)), dma((n,)), dma((9,)), dma((9,)),
            dma((half,)), dma((half,)), dma((half,)), dma((half,)), dma((half,)), dma((half,)), dma((half,)),
            dma((half, 7)), dma((half,)), dma((half,)), dma((2, 3)),
        ],
        compiler_params=pltpu.CompilerParams(collective_id=0, has_side_effects=True, vmem_limit_bytes=VMEM_LIMIT),
    )(tokens, out_grad, info, w_gate[0], w_up[0], w_down[0])
    return (d_tok, d_gate[None], d_up[None], d_down[None])


def solution(mesh):
    rows = P(("dp", "expert"), None)
    weights = P("expert", "dp", None)
    return jax.shard_map(
        per_device,
        mesh=mesh,
        in_specs=(rows, rows, rows, rows, weights, weights, weights),
        out_specs=(rows, weights, weights, weights),
        check_vma=False,
    )
```

time: 484 us -> 221 us (0.46); the launches traced: 475 us -> 220 us
  Pallas kernels: 0 us -> 209 us
  waiting for transfers between devices: 200 us -> 0 us
  blocking collectives: 121 us -> 0 us
  matrix products: 64.6 us -> 0 us
  local copies, waits for them, and re-layouts: 62.1 us -> 7.82 us
  between operations: 14.4 us -> 0.67 us
  starting transfers between devices: 11.7 us -> 0 us
    pallas_call x0 -> x1, Pallas kernels: none -> 209 us  [per_device(): pl.pallas_call(layer, out_shape=(shape((TOK, width), BF16),) + (shape((hi...]
    all_to_all x2 -> x0, blocking collectives: 121 us -> none  [the longest x1 64 us: per_device(): lax.all_to_all(input_send, 'expert', split_axis=0, concat_axis=0, tiled=T...]
    all_gather x2 -> x0, waiting for transfers between devices: 84.4 us -> none  [the longest x1 65.9 us: per_device(): lax.all_gather(grad_recv, 'dp', axis=1, tiled=True)]
    reduce_scatter x1 -> x0, waiting for transfers between devices: 84.3 us -> none  [per_device(): lax.psum_scatter(held.astype(jnp.bfloat16), 'dp', scatter_dimension=1, ti...]
    dot_general x11 -> x0, matrix products: 64.6 us -> none  [the longest x1 11.4 us: per_device(): jnp.einsum('rf,fd->rd', d_up_act, up_w, preferred_element_type=jnp.float32)]
    all_to_all x1 -> x0, waiting for transfers between devices: 31.7 us -> none  [per_device(): lax.all_to_all(slot_total[:, 0].astype(jnp.bfloat16), 'expert', split_axi...]
    all_gather x2 -> x0, local copies, waits for them, and re-layouts: 22.8 us -> none  [the longest x1 11.6 us: per_device(): lax.all_gather(grad_recv, 'dp', axis=1, tiled=True)]
    reshape x2 -> x0, local copies, waits for them, and re-layouts: 13.4 us -> none  [the longest x1 13.3 us: per_device(): partial_sum.astype(jnp.bfloat16)]
  transfers between devices with their start and end apart: 4 -> 0, of which waited for: 4 -> 0; matrix products, arithmetic and copies ran while one was open for 10% -> 0% of each run, Pallas kernels for 0% -> 0%
where the time goes in v3:
time: 221 us; the launch traced here: 220 us
  Pallas kernels  209 us (95%)
  local copies, waits for them, and re-layouts  7.82 us (4%)
    pallas_call x1, Pallas kernels, per_device(): pl.pallas_call(layer, out_shape=(shape((TOK, width), BF16),) + (shape((hi...  209 us
    unnamed x8, local copies, waits for them, and re-layouts  7.56 us

profile of v3, /device:TPU:1, one launch (start us, length us, event | category | flops | bytes accessed | tf_op | source)
XLA Modules:
  0.0 219.9 jit_solution(7618951286146925769)
XLA Ops:
  0.7 0.1 iota.11
  0.7 0.1 iota.12
  0.8 0.7 fusion.3
  1.5 0.7 fusion.2
  2.2 0.1 broadcast_in_dim.25
  2.3 0.6 broadcast_select_fusion.info
  2.9 209.5 %shard_map.102 = (bf16[24,4096]{1,0:T(8,128)(2,1)}, bf16[192,4096]{1,0:T(8,128)(2,1)}, bf16[192,4096]{1,0:T(8,128)(2,1)}, bf16[192,4096]{1,0:T(8,128)(2,1)}) custom-call(bf16[24,4096]{1,0:T(8,128)(2,1)} %tok.1, bf16[24,4096]{1,0:T(8,128)(2,1)} %ograd.1, bf16[16,128]{1,0:T(8,128)(2,1)} %broadcast_select_fusion.info, bf16[192,4096]{1,0:T(8,128)(2,1)} %bitcast.12, ...), custom_call_target="tpu_custom_call" | custom-call | tf_op jit(solution)/shard_map/pallas_call | solution.py:464
  212.4 1.6 copy.15
  214.0 0.0 copy-start.1
  214.0 2.8 %copy.16 = bf16[1,192,4096]{2,1,0:T(8,128)(2,1)} copy(bf16[1,192,4096]{2,1,0:T(8,128)(2,1)} %bitcast.11) | data formatting | bytes 3145728
  216.8 0.0 copy-done.1
  216.8 0.0 copy-start
  216.8 1.1 copy.17
  218.0 0.8 copy-done
  218.8 1.1 copy.18
  (2 shorter events, 0.0 us)
Async XLA Ops:
  214.0 2.8 %copy-start.1 = (bf16[192,4096]{1,0:T(8,128)(2,1)S(1)}, bf16[192,4096]{1,0:T(8,128)(2,1)}, u32[]{:S(2)}) copy-start(bf16[192,4096]{1,0:T(8,128)(2,1)} %get-tuple-element.10) | copy-start | bytes 4718596
  216.8 2.0 copy-start

commit v4 on v3

--- a/solution.py
+++ b/solution.py
@@ -17,8 +17,8 @@
 ROWS = NZ * CAP
 QUARTER = SRC * ROWS
 WIDTH = 256
-LAG, LATE_LAG = 2, 5
-RLATE_LAG, RLAG = 4, 2
+FAR, SELECT, LATE, MULTIPLY = 2, 4, 6, 11
+SUM, TOKENS, RFAR, END, OUT = 4, 6, 8, 10, 16
 DW_LAG = 2
 REAL = pl.ds(0, TOK)
 
@@ -56,7 +56,7 @@
         sem = pltpu.get_barrier_semaphore()
         peers = [self.at(y=self.first(self.y)), self.at(y=self.second(self.y)), self.at(c=1 - self.c)]
         peers += [self.at(z=self.zz(d)) for d in (1, -1, 2, -2)]
-        for x in (self.first(self.x), self.second(self.x)):
+        for x in (self.first(self.x), self.second(self.x), lax.rem(self.x + 2, NX)):
             peers += [self.at(x=x, c=0), self.at(x=x, c=1)]
         for p in peers:
             pl.semaphore_signal(sem, inc=1, device_id=p, device_id_type=MESH)
@@ -81,18 +81,12 @@
     return lax.dot_general(a, b, (dims, ((), ())), preferred_element_type=F32)
 
 
-def slot_exchange(p, s, sel, fwd, into, send_sem, fwd_recv, recv_sem):
+def slot_exchange(p, sel, into, send_sem, recv_sem):
     mine = p.c
-    send(sel.at[:, pl.ds(6, 2)], fwd, send_sem, fwd_recv, p.at(x=p.pick(p.x, s)))
-    for d, x in ((1, p.first(p.x)), (2, p.second(p.x))):
+    for d, x in ((3, lax.rem(p.x + 2, NX)), (1, p.first(p.x)), (2, p.second(p.x))):
         for c in range(NCORE):
             send(sel.at[:, d * 2 + c], into.at[:, d * 2 + mine], send_sem, recv_sem, p.at(x=x, c=c))
     send(sel.at[:, 1 - mine], into.at[:, mine], send_sem, recv_sem, p.at(c=1 - mine))
-
-
-def pass_on(p, s, fwd, into, fwd_send, recv_sem):
-    for c in range(NCORE):
-        send(fwd.at[:, c], into.at[:, 6 + p.c], fwd_send, recv_sem, p.at(x=p.pick(p.x, 1 - s), c=c))
 
 
 def gather_near(p, block, ssem, rsem):
@@ -154,11 +148,11 @@
         st[role] = sm[0, role].astype(F32).T.astype(BF16)
 
 
-def layer(tok, ograd, info, wg, wu, wd, d_tok, d_gate, d_up, d_down,
-          zbuf, sel, fwd, rows, wgu, wdn, acc_gu, acc_d, sm, st, rb, act_t, act,
-          got, back, fwd2, zr, tail, tail_in, dw_gu, dw_d,
-          sem_l, a_s, a_r, z_s, z_r, x_s, x_r, f_s, f_r, l_s, l_r, r_s, r_r,
-          l2_s, l2_r, x2_s, x2_r, f2_s, f2_r, z2_s, z2_r, e_s, e_r, o_s):
+def layer(tok, ograd, info, wg, wu, wd, d_tok, d_w,
+          zbuf, sel, rows, wgu, wdn, acc_gu, acc_d, sm, st, rb, act_t, act,
+          got, back, zr, tail, tail_in, dw_gu, dw_d,
+          sem_l, a_s, a_r, z_s, z_r, x_s, x_r, l_s, l_r, r_s, r_r,
+          l2_s, l2_r, x2_s, x2_r, z2_s, z2_r, e_s, e_r, o_s):
     p = Place()
     n, w = zbuf.shape[0], zbuf.shape[-1]
     half = n // 2
@@ -203,8 +197,7 @@
     token_block = lambda i: lambda z: zbuf.at[i, :, z, REAL]
 
     def step(t, carry):
-        i_far, i_sel, i_pass, i_late = (t - k * LAG for k in range(1, 5))
-        i_mul = t - 4 * LAG - LATE_LAG
+        i_far, i_sel, i_late, i_mul = t - FAR, t - SELECT, t - LATE, t - MULTIPLY
 
         @pl.when(t == 0)
         def _():
@@ -214,11 +207,11 @@
             gather_near(p, info_block, lambda j: r_s.at[j], r_r)
             await_(tok, sem_l.at[1])
 
-        @pl.when(t == LAG)
+        @pl.when(t == FAR)
         def _():
             gather_far(p, 0, info_block, lambda j: r_s.at[j], r_r)
 
-        @pl.when(t == 2 * LAG)
+        @pl.when(t == SELECT)
         def _():
             gather_wait(p, info_block, r_r)
             select_matrices(p, rb, sm, st)
@@ -244,13 +237,8 @@
             for ys, role in ((0, 0), (1, 1 + s)):
                 chosen = dot(sm[which, role], zbuf[i_sel, ys].reshape(NZ * PAD, w)).astype(BF16)
                 sel[i_sel, ys] = chosen.reshape(SRC, ROWS, w)
-            slot_exchange(p, s, sel.at[i_sel], fwd.at[i_sel], rows.at[i_sel, 0], x_s.at[i_sel], f_r.at[i_sel], x_r.at[i_sel])
+            slot_exchange(p, sel.at[i_sel], rows.at[i_sel, 0], x_s.at[i_sel], x_r.at[i_sel])
             rows[i_sel, 0, :, p.c] = sel[i_sel, :, p.c]
-
-        @when(i_pass, n)
-        def _():
-            await_(fwd.at[i_pass], f_r.at[i_pass])
-            pass_on(p, lax.rem(i_pass, 2), fwd.at[i_pass], rows.at[i_pass, 0], f_s.at[i_pass], x_r.at[i_pass])
 
         @when(i_late, n)
         def _():
@@ -285,7 +273,7 @@
 
         return carry
 
-    lax.fori_loop(0, n + 4 * LAG + LATE_LAG, step, 0)
+    lax.fori_loop(0, n + MULTIPLY, step, 0)
 
     for q in range(4):
         at = pl.ds(q * qr, qr)
@@ -320,7 +308,7 @@
         return sel.at[half + i]
 
     def back_step(t, carry):
-        i_sum, i_pass, i_tok, i_far, i_end, i_out = (t - RLATE_LAG - k * RLAG for k in range(6))
+        i_sum, i_tok, i_far, i_end, i_out = t - SUM, t - TOKENS, t - RFAR, t - END, t - OUT
         i_dw = t - DW_LAG
 
         @when(t, half)
@@ -339,17 +327,11 @@
 
         @when(i_sum, half)
         def _():
-            s = lax.rem(i_sum, 2)
             await_(got.at[i_sum], l2_r.at[i_sum])
             total = keep(i_sum)
             total[...] = (total[...].astype(F32) + got[i_sum].astype(F32)).astype(BF16)
-            slot_exchange(p, s, total, fwd2.at[i_sum], back.at[i_sum], x2_s.at[i_sum], f2_r.at[i_sum], x2_r.at[i_sum])
+            slot_exchange(p, total, back.at[i_sum], x2_s.at[i_sum], x2_r.at[i_sum])
             back[i_sum, :, p.c] = total[:, p.c]
-
-        @when(i_pass, half)
-        def _():
-            await_(fwd2.at[i_pass], f2_r.at[i_pass])
-            pass_on(p, lax.rem(i_pass, 2), fwd2.at[i_pass], back.at[i_pass], f2_s.at[i_pass], x2_r.at[i_pass])
 
         def z_send(i, j, src, d):
             send(src, zr.at[i, j], z2_s.at[i], z2_r.at[i, j], p.at(z=p.zz(d)))
@@ -401,9 +383,9 @@
             slot = lax.rem(i_dw, 2)
             at = cols(i_dw)
             copies = (
-                pltpu.make_async_copy(dw_gu.at[slot, pl.ds(0, hid)], d_gate.at[:, at], o_s.at[slot, 0]),
-                pltpu.make_async_copy(dw_gu.at[slot, pl.ds(hid, hid)], d_up.at[:, at], o_s.at[slot, 1]),
-                pltpu.make_async_copy(dw_d.at[slot], d_down.at[:, at], o_s.at[slot, 2]),
+                pltpu.make_async_copy(dw_gu.at[slot, pl.ds(0, hid)], d_w.at[pl.ds(0, hid), at], o_s.at[slot, 0]),
+                pltpu.make_async_copy(dw_gu.at[slot, pl.ds(hid, hid)], d_w.at[pl.ds(hid, hid), at], o_s.at[slot, 1]),
+                pltpu.make_async_copy(dw_d.at[slot], d_w.at[pl.ds(2 * hid, hid), at], o_s.at[slot, 2]),
             )
 
             @pl.when(i_dw >= 2)
@@ -419,19 +401,17 @@
 
         return carry
 
-    lax.fori_loop(0, half + RLATE_LAG + 5 * RLAG, back_step, 0)
+    lax.fori_loop(0, half + OUT, back_step, 0)
 
     @pl.loop(0, n)
     def _(i):
         await_(tok.at[:, pl.ds(0, w)], a_s.at[i])
-        await_(fwd.at[i], f_s.at[i])
         await_(rows.at[i, 0], l_s.at[i])
 
     @pl.loop(0, half)
     def _(i):
         await_(part(i), l2_s.at[i])
         await_(back.at[i, :, pl.ds(0, 7)], x2_s.at[i])
-        await_(fwd2.at[i], f2_s.at[i])
         await_(zr.at[i], z2_s.at[i])
         await_(tail_in.at[i], e_s.at[i])
 
@@ -461,15 +441,14 @@
     vmem = pl.BlockSpec(memory_space=pltpu.VMEM)
     dma = pltpu.SemaphoreType.DMA
     shape = jax.ShapeDtypeStruct
-    d_tok, d_gate, d_up, d_down = pl.pallas_call(
+    d_tok, d_w = pl.pallas_call(
         layer,
-        out_shape=(shape((TOK, width), BF16),) + (shape((hid, width), BF16),) * 3,
+        out_shape=(shape((TOK, width), BF16), shape((3 * hid, width), BF16)),
         in_specs=[anywhere, anywhere, vmem, anywhere, anywhere, anywhere],
-        out_specs=(vmem, anywhere, anywhere, anywhere),
+        out_specs=(vmem, anywhere),
         scratch_shapes=[
             pltpu.VMEM((n, 2, NZ, PAD, w), BF16),
             pltpu.VMEM((n, 2, SRC, ROWS, w), BF16),
-            pltpu.VMEM((n, 2, 2, ROWS, w), BF16),
             pltpu.VMEM((n, 2, 2, SRC, ROWS, w), BF16),
             pltpu.VMEM((2 * hid, width), BF16),
             pltpu.VMEM((hid, width), BF16),
@@ -482,20 +461,19 @@
             pltpu.VMEM((4 * qr, 2 * hid), BF16),
             pltpu.VMEM((half, 2, SRC, ROWS, w), BF16),
             pltpu.VMEM((half, 2, SRC, ROWS, w), BF16),
-            pltpu.VMEM((half, 2, 2, ROWS, w), BF16),
             pltpu.VMEM((half, 7, 2, TOK, w), BF16),
             pltpu.VMEM((half, 2, TOK, w), BF16),
             pltpu.VMEM((half, TOK, w), BF16),
             pltpu.VMEM((2, 2 * hid, w), BF16),
             pltpu.VMEM((2, hid, w), BF16),
             dma((6,)), dma((n,)), dma((n,)), dma((n,)), dma((n, 7)), dma((n,)), dma((n,)), dma((n,)), dma((n,)),
-            dma((n,)), dma((n,)), dma((9,)), dma((9,)),
-            dma((half,)), dma((half,)), dma((half,)), dma((half,)), dma((half,)), dma((half,)), dma((half,)),
+            dma((9,)), dma((9,)),
+            dma((half,)), dma((half,)), dma((half,)), dma((half,)), dma((half,)),
             dma((half, 7)), dma((half,)), dma((half,)), dma((2, 3)),
         ],
         compiler_params=pltpu.CompilerParams(collective_id=0, has_side_effects=True, vmem_limit_bytes=VMEM_LIMIT),
     )(tokens, out_grad, info, w_gate[0], w_up[0], w_down[0])
-    return (d_tok, d_gate[None], d_up[None], d_down[None])
+    return (d_tok, d_w[None, 0:hid], d_w[None, hid : 2 * hid], d_w[None, 2 * hid :])
 
 
 def solution(mesh):

time: 221 us -> 208 us (0.941)
  Pallas kernels: 209 us -> 199 us
    pallas_call x1, Pallas kernels: 209 us -> 199 us  [per_device(): pl.pallas_call(layer, out_shape=(shape((TOK, width), BF16), shape((3 * hi...]
    unnamed x8 -> x3, local copies, waits for them, and re-layouts: 7.56 us -> 0.68 us
    broadcast_in_dim x0 -> x1, local copies, waits for them, and re-layouts: none -> 4.72 us  [per_device(): d_w[None, 2 * hid:]]
where the time goes in v4:
time: 208 us; the launch traced here: 207 us
  Pallas kernels  199 us (96%)
  local copies, waits for them, and re-layouts  5.67 us (3%)
    pallas_call x1, Pallas kernels, per_device(): pl.pallas_call(layer, out_shape=(shape((TOK, width), BF16), shape((3 * hi...  199 us
    broadcast_in_dim x1, local copies, waits for them, and re-layouts, per_device(): d_w[None, 2 * hid:]  4.72 us

profile of v4, /device:TPU:1, one launch (start us, length us, event | category | flops | bytes accessed | tf_op | source)
XLA Modules:
  0.0 207.1 jit_solution(12676163992241468737)
XLA Ops:
  0.7 0.1 iota.11
  0.7 0.1 iota.12
  0.8 0.7 fusion.3
  1.5 0.7 fusion.2
  2.2 0.1 broadcast_in_dim.25
  2.3 0.6 broadcast_select_fusion.info
  2.9 198.7 %shard_map.102 = (bf16[24,4096]{1,0:T(8,128)(2,1)}, bf16[576,4096]{1,0:T(8,128)(2,1)}) custom-call(bf16[24,4096]{1,0:T(8,128)(2,1)} %tok.1, bf16[24,4096]{1,0:T(8,128)(2,1)} %ograd.1, bf16[16,128]{1,0:T(8,128)(2,1)} %broadcast_select_fusion.info, bf16[192,4096]{1,0:T(8,128)(2,1)} %bitcast.12, bf16[192,4096]{1,0:T(8,128)(2,1)} %bitcast.13, ...), custom_call_target="tpu_custom_call" | custom-call | tf_op jit(solution)/shard_map/pallas_call | solution.py:444
  201.6 0.0 copy-start
  201.7 4.7 %slice_bitcast_fusion = (bf16[1,192,4096]{2,1,0:T(8,128)(2,1)}, bf16[1,192,4096]{2,1,0:T(8,128)(2,1)}, bf16[1,192,4096]{2,1,0:T(8,128)(2,1)}) fusion(bf16[576,4096]{1,0:T(8,128)(2,1)} %get-tuple-element.7), kind=kLoop, calls=%fused_computation | loop fusion | bytes 9437184 | tf_op jit(solution)/shard_map/broadcast_in_dim | solution.py:476
  206.4 0.0 copy-done
  206.4 0.7 copy.12
  (2 shorter events, 0.0 us)
Async XLA Ops:
  201.6 4.7 %copy-start = (bf16[24,4096]{1,0:T(8,128)(2,1)S(1)}, bf16[24,4096]{1,0:T(8,128)(2,1)}, u32[]{:S(2)}) copy-start(bf16[24,4096]{1,0:T(8,128)(2,1)} %get-tuple-element.15) | copy-start | bytes 589828

commit v5 on v4

--- a/solution.py
+++ b/solution.py
@@ -18,7 +18,7 @@
 QUARTER = SRC * ROWS
 WIDTH = 256
 FAR, SELECT, LATE, MULTIPLY = 2, 4, 6, 11
-SUM, TOKENS, RFAR, END, OUT = 4, 6, 8, 10, 16
+SUM, TOKENS, RFAR, END, OUT = 4, 6, 8, 10, 14
 DW_LAG = 2
 REAL = pl.ds(0, TOK)
 
@@ -199,6 +199,12 @@
     def step(t, carry):
         i_far, i_sel, i_late, i_mul = t - FAR, t - SELECT, t - LATE, t - MULTIPLY
 
+        @when(i_late, n)
+        def _():
+            await_(rows.at[i_late, 0, :, pl.ds(0, 7)], x_r.at[i_late])
+            late = p.at(y=p.pick(p.y, 1 - lax.rem(i_late, 2)))
+            send(rows.at[i_late, 0], rows.at[i_late, 1], l_s.at[i_late], l_r.at[i_late], late)
+
         @pl.when(t == 0)
         def _():
             own_info.wait()
@@ -215,19 +221,6 @@
         def _():
             gather_wait(p, info_block, r_r)
             select_matrices(p, rb, sm, st)
-
-        @when(t, n)
-        def _():
-            @pl.when(t == half)
-            def _():
-                await_(ograd, sem_l.at[2])
-
-            await_(tok.at[:, pl.ds(0, w)], a_r.at[t])
-            gather_near(p, token_block(t), lambda j: z_s.at[t], z_r.at[t])
-
-        @when(i_far, n)
-        def _():
-            gather_far(p, lax.rem(i_far, 2), token_block(i_far), lambda j: z_s.at[i_far], z_r.at[i_far])
 
         @when(i_sel, n)
         def _():
@@ -240,11 +233,18 @@
             slot_exchange(p, sel.at[i_sel], rows.at[i_sel, 0], x_s.at[i_sel], x_r.at[i_sel])
             rows[i_sel, 0, :, p.c] = sel[i_sel, :, p.c]
 
-        @when(i_late, n)
-        def _():
-            await_(rows.at[i_late, 0, :, pl.ds(0, 7)], x_r.at[i_late])
-            late = p.at(y=p.pick(p.y, 1 - lax.rem(i_late, 2)))
-            send(rows.at[i_late, 0], rows.at[i_late, 1], l_s.at[i_late], l_r.at[i_late], late)
+        @when(i_far, n)
+        def _():
+            gather_far(p, lax.rem(i_far, 2), token_block(i_far), lambda j: z_s.at[i_far], z_r.at[i_far])
+
+        @when(t, n)
+        def _():
+            @pl.when(t == half)
+            def _():
+                await_(ograd, sem_l.at[2])
+
+            await_(tok.at[:, pl.ds(0, w)], a_r.at[t])
+            gather_near(p, token_block(t), lambda j: z_s.at[t], z_r.at[t])
 
         @pl.when(i_mul == 0)
         def _():
@@ -255,6 +255,9 @@
         def _():
             s = lax.rem(i_mul, 2)
             await_(rows.at[i_mul, 1], l_r.at[i_mul])
+            await_(tok.at[:, pl.ds(0, w)], a_s.at[i_mul])
+            await_(zbuf.at[i_mul, :, pl.ds(0, 7), REAL], z_s.at[i_mul])
+            await_(sel.at[i_mul, :, pl.ds(0, 7)], x_s.at[i_mul])
 
             def multiply(acc, weights):
                 part = weights[:, cols(lax.rem(i_mul, half))]
@@ -290,11 +293,6 @@
             act_t[order, 0 : 2 * hid, to] = both
             act_t[order, 2 * hid : 3 * hid, to] = hidden
 
-    @pl.loop(0, n)
-    def _(i):
-        await_(zbuf.at[i, :, pl.ds(0, 7), REAL], z_s.at[i])
-        await_(sel.at[i, :, pl.ds(0, 7)], x_s.at[i])
-
     def part(i):
         return zbuf.at[i]
 
@@ -355,6 +353,7 @@
             s = lax.rem(i_far, 2)
             for j in range(3):
                 await_(zr.at[i_far, j], z2_r.at[i_far, j])
+            await_(part(i_far), l2_s.at[i_far])
             four = zr[i_far, 2].astype(F32)
             for j, d in enumerate((-2, 2)):
                 value = own(i_far)[:, p.zz(d), REAL].astype(F32) + zr[i_far, j].astype(F32)
@@ -366,6 +365,7 @@
         def _():
             for j in range(3, 7):
                 await_(zr.at[i_end, j], z2_r.at[i_end, j])
+            await_(back.at[i_end, :, pl.ds(0, 7)], x2_s.at[i_end])
             value = own(i_end)[:, p.z, REAL].astype(F32)
             for j in range(3, 7):
                 value = value + zr[i_end, j].astype(F32)
@@ -375,6 +375,8 @@
         @when(i_out, half)
         def _():
             await_(tail_in.at[i_out], e_r.at[i_out])
+            await_(zr.at[i_out], z2_s.at[i_out])
+            await_(tail_in.at[i_out], e_s.at[i_out])
             value = tail[i_out, 0].astype(F32) + tail_in[i_out].astype(F32)
             d_tok[:, cols(i_out)] = value.astype(BF16)
 
@@ -382,6 +384,8 @@
         def _():
             slot = lax.rem(i_dw, 2)
             at = cols(i_dw)
+            for k in (i_dw, half + i_dw):
+                await_(rows.at[k, 0], l_s.at[k])
             copies = (
                 pltpu.make_async_copy(dw_gu.at[slot, pl.ds(0, hid)], d_w.at[pl.ds(0, hid), at], o_s.at[slot, 0]),
                 pltpu.make_async_copy(dw_gu.at[slot, pl.ds(hid, hid)], d_w.at[pl.ds(hid, hid), at], o_s.at[slot, 1]),
@@ -402,18 +406,6 @@
         return carry
 
     lax.fori_loop(0, half + OUT, back_step, 0)
-
-    @pl.loop(0, n)
-    def _(i):
-        await_(tok.at[:, pl.ds(0, w)], a_s.at[i])
-        await_(rows.at[i, 0], l_s.at[i])
-
-    @pl.loop(0, half)
-    def _(i):
-        await_(part(i), l2_s.at[i])
-        await_(back.at[i, :, pl.ds(0, 7)], x2_s.at[i])
-        await_(zr.at[i], z2_s.at[i])
-        await_(tail_in.at[i], e_s.at[i])
 
     for slot in range(2):
         for j in range(3):
@@ -433,9 +425,11 @@
     qr = QUARTER
     z = lax.rem(lax.div(lax.axis_index("expert"), NCORE), NZ)
 
-    info = jnp.concatenate([(routes + 1).astype(BF16).T, gates.T], axis=0)
-    info = jnp.pad(info, ((0, 0), (0, PAD - TOK)))
-    info = jnp.where(lax.broadcasted_iota(jnp.int32, (16, 4, PAD), 1) == lax.rem(z, 4), info[:, None, :], 0).reshape(16, 128)
+    both = jnp.concatenate([(routes + 1).astype(BF16), gates], axis=1)
+    token = lax.broadcasted_iota(jnp.int32, (TOK, 128), 0)
+    lane = lax.broadcasted_iota(jnp.int32, (TOK, 128), 1)
+    to_lane = (lane == token + PAD * lax.rem(z, 4)).astype(BF16)
+    info = dot(both, to_lane, ((0,), (0,))).astype(BF16)
 
     anywhere = pl.BlockSpec(memory_space=pl.ANY)
     vmem = pl.BlockSpec(memory_space=pltpu.VMEM)

time: 208 us -> 206 us (level)
  no operation moved by 1% of the time
where the time goes in v5:
time: 206 us
  Pallas kernels  198 us (96%)
  local copies, waits for them, and re-layouts  5.41 us (3%)
    pallas_call x1, Pallas kernels, per_device(): pl.pallas_call(layer, out_shape=(shape((TOK, width), BF16), shape((3 * hi...  198 us
    broadcast_in_dim x1, local copies, waits for them, and re-layouts, per_device(): d_w[None, 2 * hid:]  4.72 us

profile of v5, /device:TPU:1, one launch (start us, length us, event | category | flops | bytes accessed | tf_op | source)
XLA Modules:
  0.0 205.9 jit_solution(4436974839515600419)
XLA Ops:
  0.7 0.7 add_convert_fusion
  1.4 1.5 convolution_convert_fusion.info
  2.8 197.6 %shard_map.102 = (bf16[24,4096]{1,0:T(8,128)(2,1)}, bf16[576,4096]{1,0:T(8,128)(2,1)}) custom-call(bf16[24,4096]{1,0:T(8,128)(2,1)} %tok.1, bf16[24,4096]{1,0:T(8,128)(2,1)} %ograd.1, bf16[16,128]{1,0:T(8,128)(2,1)} %convolution_convert_fusion.info, bf16[192,4096]{1,0:T(8,128)(2,1)} %bitcast.9, bf16[192,4096]{1,0:T(8,128)(2,1)} %bitcast.10, ...), custom_call_target="tpu_custom_call" | custom-call | tf_op jit(solution)/shard_map/pallas_call | solution.py:438
  200.5 0.0 copy-start
  200.5 4.7 %slice_bitcast_fusion = (bf16[1,192,4096]{2,1,0:T(8,128)(2,1)}, bf16[1,192,4096]{2,1,0:T(8,128)(2,1)}, bf16[1,192,4096]{2,1,0:T(8,128)(2,1)}) fusion(bf16[576,4096]{1,0:T(8,128)(2,1)} %get-tuple-element.7), kind=kLoop, calls=%fused_computation | loop fusion | bytes 9437184 | tf_op jit(solution)/shard_map/broadcast_in_dim | solution.py:470
  205.2 0.0 copy-done
  205.2 0.7 copy.12
  (1 shorter events, 0.0 us)
Async XLA Ops:
  200.5 4.7 %copy-start = (bf16[24,4096]{1,0:T(8,128)(2,1)S(1)}, bf16[24,4096]{1,0:T(8,128)(2,1)}, u32[]{:S(2)}) copy-start(bf16[24,4096]{1,0:T(8,128)(2,1)} %get-tuple-element.15) | copy-start | bytes 589828
